TPU v7x, 32 devices: a whole 2x2x4 slice. The times are simulated.
32 devices in a mesh: dp: 32 (over z, y, x, core).
Axes of the slice: x: 2, y: 2, z: 4, core: 2. Of those that a mesh axis runs over, the one named last changes fastest.
Arguments:
- series: bfloat16 [32, 288, 512], P('dp'), may hold values from -6 to 6
- horizon: int32 [32], P('dp'), may hold values from 0 to 3
- cotangent: bfloat16 [32, 288, 512], P('dp'), may hold values from -6 to 6
- fine_down: bfloat16 [12, 262144], replicated, may hold values from -0.078125 to 0.078125
- fine_down_bias: bfloat16 [512], replicated, may hold values from -3 to 3
- fine_isometric: bfloat16 [25, 262144], replicated, may hold values from -0.0546875 to 0.0546875
- fine_isometric_bias: bfloat16 [512], replicated, may hold values from -3 to 3
- fine_upsample: bfloat16 [12, 262144], replicated, may hold values from -0.25 to 0.25
- fine_upsample_bias: bfloat16 [512], replicated, may hold values from -3 to 3
- coarse_down: bfloat16 [16, 262144], replicated, may hold values from -0.0625 to 0.0625
- coarse_down_bias: bfloat16 [512], replicated, may hold values from -3 to 3
- coarse_isometric: bfloat16 [19, 262144], replicated, may hold values from -0.0625 to 0.0625
- coarse_isometric_bias: bfloat16 [512], replicated, may hold values from -3 to 3
- coarse_upsample: bfloat16 [16, 262144], replicated, may hold values from -0.25 to 0.25
- coarse_upsample_bias: bfloat16 [512], replicated, may hold values from -3 to 3
- branch_gain: bfloat16 [512], replicated, may hold values from 0.099609375 to 1.8984375
- branch_bias: bfloat16 [512], replicated, may hold values from -3 to 3
- merge_weight: bfloat16 [2, 262144], replicated, may hold values from -0.1875 to 0.1875
- merge_bias: bfloat16 [512], replicated, may hold values from -3 to 3
- first_gain: bfloat16 [512], replicated, may hold values from 0.099609375 to 1.8984375
- first_bias: bfloat16 [512], replicated, may hold values from -3 to 3
- expand_weight: bfloat16 [512, 2048], replicated, may hold values from -0.25 to 0.25
- expand_bias: bfloat16 [2048], replicated, may hold values from -3 to 3
- reduce_weight: bfloat16 [2048, 512], replicated, may hold values from -0.125 to 0.125
- reduce_bias: bfloat16 [512], replicated, may hold values from -3 to 3
- final_gain: bfloat16 [512], replicated, may hold values from 0.099609375 to 1.8984375
- final_bias: bfloat16 [512], replicated, may hold values from -3 to 3
Outputs:
- result: float32 [32, 288, 512], P('dp')
- series_gradient: float32 [32, 288, 512], P('dp')
- fine_down_gradient: float32 [12, 262144], P(None, 'dp')
- fine_down_bias_gradient: float32 [512], replicated
- fine_isometric_gradient: float32 [25, 262144], P(None, 'dp')
- fine_isometric_bias_gradient: float32 [512], replicated
- fine_upsample_gradient: float32 [12, 262144], P(None, 'dp')
- fine_upsample_bias_gradient: float32 [512], replicated
- coarse_down_gradient: float32 [16, 262144], P(None, 'dp')
- coarse_down_bias_gradient: float32 [512], replicated
- coarse_isometric_gradient: float32 [19, 262144], P(None, 'dp')
- coarse_isometric_bias_gradient: float32 [512], replicated
- coarse_upsample_gradient: float32 [16, 262144], P(None, 'dp')
- coarse_upsample_bias_gradient: float32 [512], replicated
- branch_gain_gradient: float32 [512], replicated
- branch_bias_gradient: float32 [512], replicated
- merge_weight_gradient: float32 [2, 262144], P(None, 'dp')
- merge_bias_gradient: float32 [512], replicated
- first_gain_gradient: float32 [512], replicated
- first_bias_gradient: float32 [512], replicated
- expand_weight_gradient: float32 [512, 2048], P(None, 'dp')
- expand_bias_gradient: float32 [2048], replicated
- reduce_weight_gradient: float32 [2048, 512], P('dp')
- reduce_bias_gradient: float32 [512], replicated
- final_gain_gradient: float32 [512], replicated
- final_bias_gradient: float32 [512], replicated
Inputs may be any that keep to these rules, and one draw needn't show every extreme that they name: A series' valid steps are the first 288 * (192, 288, 432, 816)[horizon] / 816.
All inputs are finite; a program needn't handle non-finite values.
Results may differ from a plain program's by a relative error of at most 0.014.
Values may be sent and summed in bfloat16 or wider, within the bound.
A program may use at most 384 MiB of HBM per device.

v0:
```python
from functools import partial

import jax
import jax.numpy as jnp
from jax import lax
from jax.sharding import PartitionSpec as P

K_A = 12
K_B = 16


EPSILON = 1e-05
HORIZON_ENDS = (192, 288, 432, 816)
FLOAT = jnp.float32
BFLOAT = jnp.bfloat16


def moving_trend(values, window):
    half_width = (window - 1) // 2
    axis_time = values.ndim - 2
    steps_total = values.shape[axis_time]
    widths = [(0, 0)] * axis_time + [(half_width, half_width), (0, 0)]
    padded = jnp.pad(values, widths, mode="edge")
    running = lax.slice_in_dim(padded, 0, steps_total, axis=axis_time)
    for offset in range(1, window):
        running = running + lax.slice_in_dim(padded, offset, offset + steps_total, axis=axis_time)
    return running / window


def seasonal_part(values, window):
    return values - moving_trend(values, window)


def layer_norm(values, norm_gain, norm_shift):
    average = jnp.mean(values, axis=-1, keepdims=True)
    centered = values - average
    variance = jnp.mean(centered * centered, axis=-1, keepdims=True)
    return centered * lax.rsqrt(variance + EPSILON) * norm_gain + norm_shift


def gelu_exact(values):
    return jax.nn.gelu(values, approximate=False)


def product(operand, matrix):
    return jnp.dot(operand, matrix, preferred_element_type=FLOAT)


def product_back(gradient, matrix):
    return lax.dot_general(gradient, matrix, (((1,), (1,)), ((), ())), preferred_element_type=FLOAT)


def weight_product(operand, gradient):
    return lax.dot_general(
        operand, gradient, (((0,), (0,)), ((), ())), preferred_element_type=FLOAT
    )


def column_total(gradient):
    return jnp.sum(gradient, axis=0, dtype=FLOAT)


def valid_masks(horizon, length_total):
    valid_ends = jnp.zeros(horizon.shape, jnp.int32)
    for number, ending in enumerate(HORIZON_ENDS):
        valid_ends = valid_ends + jnp.where(horizon == number, length_total * ending, 0).astype(
            jnp.int32
        )
    positions = lax.iota(jnp.int32, length_total) * 816
    return (positions[None, :] < valid_ends[:, None]).astype(FLOAT)


def unfold_rows(values):
    batch_count, step_count, channels = values.shape
    padded_steps = 2 * step_count - 1
    padded = jnp.pad(values, ((0, 0), (step_count - 1, 0), (0, 0)))
    tiled = jnp.broadcast_to(padded[:, None], (batch_count, step_count + 1, padded_steps, channels))
    tiled = tiled.reshape(batch_count, (step_count + 1) * padded_steps, channels)
    tiled = tiled[:, : step_count * (padded_steps + 1)].reshape(
        batch_count, step_count, padded_steps + 1, channels
    )
    return tiled[:, :, :step_count]


def fold_rows(blocks):
    batch_count = blocks.shape[0]
    step_count = blocks.shape[1]
    channels = blocks.shape[3]
    widened = jnp.pad(blocks, ((0, 0), (0, 0), (0, step_count), (0, 0)))
    widened = widened.reshape(batch_count, 2 * step_count * step_count, channels)
    widened = widened[:, : step_count * (2 * step_count - 1)].reshape(
        batch_count, step_count, 2 * step_count - 1, channels
    )
    return jnp.sum(widened, axis=1)[:, step_count - 1 :]


def branch_forward(series32, params, kernel, norm_gain, norm_shift):
    down_weight, down_bias, isometric_weight, isometric_bias, upsample_weight, upsample_bias = (
        params
    )
    batch_count, length_total, channels = series32.shape
    step_count = length_total // kernel + 1
    half_kernel = kernel // 2
    season, season_pull = jax.vjp(partial(seasonal_part, window=kernel + 1), series32)
    padded = jnp.pad(season.astype(BFLOAT), ((0, 0), (half_kernel, half_kernel), (0, 0)))
    patches = padded.reshape(batch_count * step_count, kernel * channels)
    down_out = jnp.tanh(
        product(patches, down_weight.reshape(kernel * channels, channels)) + down_bias.astype(FLOAT)
    )
    down_low = down_out.astype(BFLOAT).reshape(batch_count, step_count, channels)
    unfolded = unfold_rows(down_low).reshape(batch_count * step_count, step_count * channels)
    iso_out = jnp.tanh(
        product(unfolded, isometric_weight.reshape(step_count * channels, channels))
        + isometric_bias.astype(FLOAT)
    )
    joined, inner_pull = jax.vjp(layer_norm, iso_out + down_out, norm_gain, norm_shift)
    joined_low = joined.astype(BFLOAT)
    upward = jnp.einsum(
        "sa,jab->sjb",
        joined_low,
        upsample_weight.reshape(kernel, channels, channels),
        preferred_element_type=FLOAT,
    )
    upward = upward.reshape(batch_count, step_count * kernel, channels)[:, :length_total]
    up_out = jnp.tanh(upward + upsample_bias.astype(FLOAT))
    branch_out, outer_pull = jax.vjp(layer_norm, up_out + season, norm_gain, norm_shift)
    saved_values = (
        season_pull,
        patches,
        down_out,
        down_low,
        unfolded,
        iso_out,
        inner_pull,
        joined_low,
        up_out,
        outer_pull,
    )
    return (branch_out, saved_values)


def branch_backward(grad_out, saved_values, params, kernel):
    (
        season_pull,
        patches,
        down_out,
        down_low,
        unfolded,
        iso_out,
        inner_pull,
        joined_low,
        up_out,
        outer_pull,
    ) = saved_values
    down_weight, down_bias, isometric_weight, isometric_bias, upsample_weight, upsample_bias = (
        params
    )
    batch_count, length_total, channels = up_out.shape
    step_count = length_total // kernel + 1
    half_kernel = kernel // 2
    grad_outer, gain_outer, shift_outer = outer_pull(grad_out)
    grad_up = grad_outer * (1.0 - up_out * up_out)
    grad_up = jnp.pad(grad_up, ((0, 0), (0, step_count * kernel - length_total), (0, 0)))
    grad_up_low = grad_up.astype(BFLOAT).reshape(batch_count * step_count, kernel, channels)
    upsample_bias_grad = jnp.sum(grad_up_low, axis=(0, 1), dtype=FLOAT)
    upsample_grad = jnp.einsum(
        "sa,sjb->jab", joined_low, grad_up_low, preferred_element_type=FLOAT
    ).reshape(kernel, channels * channels)
    grad_joined = jnp.einsum(
        "sjb,jab->sa",
        grad_up_low,
        upsample_weight.reshape(kernel, channels, channels),
        preferred_element_type=FLOAT,
    )
    grad_inner, gain_inner, shift_inner = inner_pull(grad_joined)
    grad_iso_low = (grad_inner * (1.0 - iso_out * iso_out)).astype(BFLOAT)
    isometric_bias_grad = column_total(grad_iso_low)
    isometric_grad = weight_product(unfolded, grad_iso_low).reshape(step_count, channels * channels)
    grad_unfolded = product_back(
        grad_iso_low, isometric_weight.reshape(step_count * channels, channels)
    )
    grad_unfolded = grad_unfolded.reshape(batch_count, step_count, step_count, channels)
    grad_down = grad_inner + fold_rows(grad_unfolded).reshape(batch_count * step_count, channels)
    grad_down_low = (grad_down * (1.0 - down_out * down_out)).astype(BFLOAT)
    down_bias_grad = column_total(grad_down_low)
    down_grad = weight_product(patches, grad_down_low).reshape(kernel, channels * channels)
    grad_patches = product_back(grad_down_low, down_weight.reshape(kernel * channels, channels))
    grad_patches = grad_patches.reshape(batch_count, step_count * kernel, channels)[
        :, half_kernel : half_kernel + length_total
    ]
    grad_series = season_pull(grad_outer + grad_patches)[0]
    gradients = (
        down_grad,
        down_bias_grad,
        isometric_grad,
        isometric_bias_grad,
        upsample_grad,
        upsample_bias_grad,
    )
    return (grad_series, gradients, gain_outer + gain_inner, shift_outer + shift_inner)


def body(
    series,
    horizon,
    cotangent,
    fine_down,
    fine_down_bias,
    fine_isometric,
    fine_isometric_bias,
    fine_upsample,
    fine_upsample_bias,
    coarse_down,
    coarse_down_bias,
    coarse_isometric,
    coarse_isometric_bias,
    coarse_upsample,
    coarse_upsample_bias,
    branch_gain,
    branch_bias,
    merge_weight,
    merge_bias,
    first_gain,
    first_bias,
    expand_weight,
    expand_bias,
    reduce_weight,
    reduce_bias,
    final_gain,
    final_bias,
):
    batch_count, length_total, channels = series.shape
    row_count = batch_count * length_total
    series32 = series.astype(FLOAT)
    mask_rows = valid_masks(horizon, length_total).reshape(row_count, 1)
    branch_gain32 = branch_gain.astype(FLOAT)
    branch_shift32 = branch_bias.astype(FLOAT)
    fine_params = (
        fine_down,
        fine_down_bias,
        fine_isometric,
        fine_isometric_bias,
        fine_upsample,
        fine_upsample_bias,
    )
    coarse_params = (
        coarse_down,
        coarse_down_bias,
        coarse_isometric,
        coarse_isometric_bias,
        coarse_upsample,
        coarse_upsample_bias,
    )
    fine_out, fine_saved = branch_forward(series32, fine_params, K_A, branch_gain32, branch_shift32)
    coarse_out, coarse_saved = branch_forward(
        series32, coarse_params, K_B, branch_gain32, branch_shift32
    )
    branch_low = jnp.concatenate(
        [fine_out.astype(BFLOAT), coarse_out.astype(BFLOAT)], axis=-1
    ).reshape(row_count, 2 * channels)
    merge_matrix = merge_weight.reshape(2 * channels, channels)
    merged = product(branch_low, merge_matrix) + merge_bias.astype(FLOAT)
    normed, first_pull = jax.vjp(
        layer_norm, merged, first_gain.astype(FLOAT), first_bias.astype(FLOAT)
    )
    normed_low = normed.astype(BFLOAT)
    expanded = product(normed_low, expand_weight) + expand_bias.astype(FLOAT)
    activated, gelu_pull = jax.vjp(gelu_exact, expanded)
    activated_low = activated.astype(BFLOAT)
    reduced = product(activated_low, reduce_weight) + reduce_bias.astype(FLOAT)
    final_out, final_pull = jax.vjp(
        layer_norm, merged + reduced, final_gain.astype(FLOAT), final_bias.astype(FLOAT)
    )
    result = (final_out * mask_rows).reshape(batch_count, length_total, channels)
    grad_result = cotangent.astype(FLOAT).reshape(row_count, channels) * mask_rows
    grad_residual, final_gain_grad, final_bias_grad = final_pull(grad_result)
    grad_reduced_low = grad_residual.astype(BFLOAT)
    reduce_bias_grad = column_total(grad_reduced_low)
    reduce_grad = weight_product(activated_low, grad_reduced_low)
    grad_activated = product_back(grad_reduced_low, reduce_weight)
    grad_expanded_low = gelu_pull(grad_activated)[0].astype(BFLOAT)
    expand_bias_grad = column_total(grad_expanded_low)
    expand_grad = weight_product(normed_low, grad_expanded_low)
    grad_normed = product_back(grad_expanded_low, expand_weight)
    grad_merged_norm, first_gain_grad, first_bias_grad = first_pull(grad_normed)
    grad_merged_low = (grad_residual + grad_merged_norm).astype(BFLOAT)
    merge_bias_grad = column_total(grad_merged_low)
    merge_grad = weight_product(branch_low, grad_merged_low).reshape(2, channels * channels)
    grad_branches = product_back(grad_merged_low, merge_matrix)
    grad_fine = grad_branches[:, :channels].reshape(batch_count, length_total, channels)
    grad_coarse = grad_branches[:, channels:].reshape(batch_count, length_total, channels)
    fine_series, fine_grads, fine_gain, fine_shift = branch_backward(
        grad_fine, fine_saved, fine_params, K_A
    )
    coarse_series, coarse_grads, coarse_gain, coarse_shift = branch_backward(
        grad_coarse, coarse_saved, coarse_params, K_B
    )
    series_gradient = fine_series + coarse_series
    (
        fine_down_bias_gradient,
        fine_isometric_bias_gradient,
        fine_upsample_bias_gradient,
        coarse_down_bias_gradient,
        coarse_isometric_bias_gradient,
        coarse_upsample_bias_gradient,
        branch_gain_gradient,
        branch_bias_gradient,
        merge_bias_gradient,
        first_gain_gradient,
        first_bias_gradient,
        expand_bias_gradient,
        reduce_bias_gradient,
        final_gain_gradient,
        final_bias_gradient,
    ) = lax.psum(
        (
            fine_grads[1],
            fine_grads[3],
            fine_grads[5],
            coarse_grads[1],
            coarse_grads[3],
            coarse_grads[5],
            fine_gain + coarse_gain,
            fine_shift + coarse_shift,
            merge_bias_grad,
            first_gain_grad,
            first_bias_grad,
            expand_bias_grad,
            reduce_bias_grad,
            final_gain_grad,
            final_bias_grad,
        ),
        "dp",
    )
    (
        fine_down_gradient,
        fine_isometric_gradient,
        fine_upsample_gradient,
        coarse_down_gradient,
        coarse_isometric_gradient,
        coarse_upsample_gradient,
        merge_weight_gradient,
        expand_weight_gradient,
        reduce_weight_gradient,
    ) = (
        lax.psum_scatter(fine_grads[0], "dp", scatter_dimension=1, tiled=True),
        lax.psum_scatter(fine_grads[2], "dp", scatter_dimension=1, tiled=True),
        lax.psum_scatter(fine_grads[4], "dp", scatter_dimension=1, tiled=True),
        lax.psum_scatter(coarse_grads[0], "dp", scatter_dimension=1, tiled=True),
        lax.psum_scatter(coarse_grads[2], "dp", scatter_dimension=1, tiled=True),
        lax.psum_scatter(coarse_grads[4], "dp", scatter_dimension=1, tiled=True),
        lax.psum_scatter(merge_grad, "dp", scatter_dimension=1, tiled=True),
        lax.psum_scatter(expand_grad, "dp", scatter_dimension=1, tiled=True),
        lax.psum_scatter(reduce_grad, "dp", scatter_dimension=0, tiled=True),
    )
    return (
        result,
        series_gradient,
        fine_down_gradient,
        fine_down_bias_gradient,
        fine_isometric_gradient,
        fine_isometric_bias_gradient,
        fine_upsample_gradient,
        fine_upsample_bias_gradient,
        coarse_down_gradient,
        coarse_down_bias_gradient,
        coarse_isometric_gradient,
        coarse_isometric_bias_gradient,
        coarse_upsample_gradient,
        coarse_upsample_bias_gradient,
        branch_gain_gradient,
        branch_bias_gradient,
        merge_weight_gradient,
        merge_bias_gradient,
        first_gain_gradient,
        first_bias_gradient,
        expand_weight_gradient,
        expand_bias_gradient,
        reduce_weight_gradient,
        reduce_bias_gradient,
        final_gain_gradient,
        final_bias_gradient,
    )


def solution(mesh):
    in_specs = (
        P("dp", None, None),
        P("dp"),
        P("dp", None, None),
        P(),
        P(),
        P(),
        P(),
        P(),
        P(),
        P(),
        P(),
        P(),
        P(),
        P(),
        P(),
        P(),
        P(),
        P(),
        P(),
        P(),
        P(),
        P(),
        P(),
        P(),
        P(),
        P(),
        P(),
    )
    out_specs = (
        P("dp", None, None),
        P("dp", None, None),
        P(None, "dp"),
        P(),
        P(None, "dp"),
        P(),
        P(None, "dp"),
        P(),
        P(None, "dp"),
        P(),
        P(None, "dp"),
        P(),
        P(None, "dp"),
        P(),
        P(),
        P(),
        P(None, "dp"),
        P(),
        P(),
        P(),
        P(None, "dp"),
        P(),
        P("dp", None),
        P(),
        P(),
        P(),
    )
    return jax.shard_map(body, mesh=mesh, in_specs=in_specs, out_specs=out_specs, check_vma=False)
```

profile of v0, /device:TPU:0, one launch (start us, length us, event | category | flops | bytes accessed | tf_op | source)
XLA Modules:
  0.0 1974.5 jit_solution(1368996326393857927)
XLA Ops:
  27.9 8.7 reshape.527
  51.4 8.3 reshape.537
  73.2 9.9 copy.84
  83.1 9.7 copy.86
  92.7 12.8 reshape.541
  114.5 13.4 reshape.531
  127.9 7.2 fusion.145
  178.6 6.4 convolution_bitcast_fusion.1
  185.0 12.6 copy.74
  197.7 12.4 pad.222
  210.1 17.8 copy.89
  227.9 17.0 copy.87
  251.1 6.8 fusion.14
  260.8 8.8 slice_reduce_fusion
  281.3 15.2 reshape.559
  296.7 10.4 copy.88
  321.2 8.1 fusion.161
  329.3 16.6 reshape.562
  346.0 8.2 convolution_bitcast_fusion
  354.1 20.2 %copy.90 = f32[2,8,512,512]{3,1,2,0:T(8,128)} copy(f32[2,8,512,512]{2,3,1,0:T(8,128)} %bitcast.174) | data formatting | bytes 33554432
  375.4 8.3 fusion.162
  383.7 23.1 %reshape.563 = f32[19,262144]{1,0:T(8,128)} reshape(f32[9728,512]{1,0:T(8,128)} %fusion.162) | data formatting | bytes 39845888 | tf_op jit(solution)/shard_map/reshape | solution.py:178
  407.9 10.7 fusion.160
  418.7 30.3 %reshape.560 = f32[25,262144]{1,0:T(8,128)} reshape(f32[12800,512]{1,0:T(8,128)} %fusion.160) | data formatting | bytes 52428800 | tf_op jit(solution)/shard_map/reshape | solution.py:178
  463.6 43.5 %all-reduce.47 = (f32[512]{0:T(512)}, f32[512]{0:T(512)}, f32[512]{0:T(512)}, f32[512]{0:T(512)}, f32[512]{0:T(512)}, /*index=5*/f32[512]{0:T(512)}, f32[512]{0:...) all-reduce(f32[512]{0:T(512)S(1)} %get-tuple-element.77, ...), channel_id=1, replica_groups=mesh['dp'=32] {'dp'}, use_global_device_ids=true, to_apply=%region_32.33 | all-reduce | flops 9216 | bytes 73728 | tf_op jit(solution)/shard_map/psum | solution.py:315
  511.5 76.3 %reduce-scatter.24.cloned.1.call-done = f32[64,512]{1,0:T(8,128)} async-done(((f32[2048,512]{1,0:T(8,128)}), f32[64,512]{1,0:T(8,128)}) %reduce-scatter.24.cloned.1.call-update) | async-done | bytes 131088 | tf_op jit(solution)/shard_map/reduce_scatter | solution.py:354
  587.8 181.5 %reduce-scatter.14.cloned.1.call-done = f32[12,8192]{1,0:T(8,128)} async-done(((f32[12,262144]{1,0:T(8,128)}), f32[12,8192]{1,0:T(8,128)}) %reduce-scatter.14.cloned.1.call-update) | async-done | bytes 393232 | tf_op jit(solution)/shard_map/reduce_scatter | solution.py:348
  769.3 187.3 %reduce-scatter.10.cloned.1.call-done = f32[12,8192]{1,0:T(8,128)} async-done(((f32[12,262144]{1,0:T(8,128)}), f32[12,8192]{1,0:T(8,128)}) %reduce-scatter.10.cloned.1.call-update) | async-done | bytes 393232 | tf_op jit(solution)/shard_map/reduce_scatter | solution.py:346
  956.7 187.4 %reduce-scatter.16.cloned.1.call-done = f32[16,8192]{1,0:T(8,128)} async-done(((f32[16,262144]{1,0:T(8,128)}), f32[16,8192]{1,0:T(8,128)}) %reduce-scatter.16.cloned.1.call-update) | async-done | bytes 524304 | tf_op jit(solution)/shard_map/reduce_scatter | solution.py:349
  1144.0 187.5 %reduce-scatter.20.cloned.1.call-done = f32[16,8192]{1,0:T(8,128)} async-done(((f32[16,262144]{1,0:T(8,128)}), f32[16,8192]{1,0:T(8,128)}) %reduce-scatter.20.cloned.1.call-update) | async-done | bytes 524304 | tf_op jit(solution)/shard_map/reduce_scatter | solution.py:351
  1331.5 272.7 %reduce-scatter.18.cloned.1.call-done = f32[19,8192]{1,0:T(8,128)} async-done(((f32[19,262144]{1,0:T(8,128)}), f32[19,8192]{1,0:T(8,128)}) %reduce-scatter.18.cloned.1.call-update) | async-done | bytes 622608 | tf_op jit(solution)/shard_map/reduce_scatter | solution.py:350
  1604.3 363.5 %reduce-scatter.12.cloned.1.call-done = f32[25,8192]{1,0:T(8,128)} async-done(((f32[25,262144]{1,0:T(8,128)}), f32[25,8192]{1,0:T(8,128)}) %reduce-scatter.12.cloned.1.call-update) | async-done | bytes 819216 | tf_op jit(solution)/shard_map/reduce_scatter | solution.py:347
  (313 shorter events, 156.0 us)
Async XLA Ops:
  7.2 137.3 %copy-start = (bf16[512,2048]{1,0:T(8,128)(2,1)S(1)}, bf16[512,2048]{1,0:T(8,128)(2,1)}, u32[]{:S(2)}) copy-start(bf16[512,2048]{1,0:T(8,128)(2,1)} %param.48) | copy-start | bytes 6291460
  7.2 502.8 %all-reduce.50.cloned.1.call-start = ((), (), s32[]{:S(2)}) async-start(), calls=%async_computation.16 | async-start | bytes 4194304
  27.7 8.9 copy-start.22
  27.9 31.8 %copy-start.12 = (bf16[19,8192]{1,0:T(8,128)(2,1)}, bf16[19,8192]{1,0:T(8,128)(2,1)S(1)}, u32[]{:S(2)}) copy-start(bf16[19,8192]{1,0:T(8,128)(2,1)S(1)} %reshape.536) | copy-start | bytes 933892
  51.4 76.5 %copy-start.5 = (bf16[4,8,25,512]{3,1,2,0:T(8,128)(2,1)}, bf16[4,8,25,512]{3,1,2,0:T(8,128)(2,1)S(1)}, u32[]{:S(2)}) copy-start(bf16[4,8,25,512]{3,1,2,0:T(8,128)(2,1)S(1)} %copy.83) | copy-start | bytes 2457604
  64.3 41.2 %copy-start.40 = (f32[19,512]{1,0:T(8,128)}, f32[19,512]{1,0:T(8,128)S(1)}, u32[]{:S(2)}) copy-start(f32[19,512]{1,0:T(8,128)S(1)} %fusion.27) | copy-start | bytes 116740
  73.2 32.3 %copy-start.10 = (bf16[3,8,19,512]{3,1,2,0:T(8,128)(2,1)}, bf16[3,8,19,512]{3,1,2,0:T(8,128)(2,1)S(1)}, u32[]{:S(2)}) copy-start(bf16[3,8,19,512]{3,1,2,0:T(8,128)(2,1)S(1)} %copy.85) | copy-start | bytes 1400836
  144.2 14.1 copy-start.14
  164.1 347.5 %reduce-scatter.22.cloned.1.call-start = ((), (), s32[]{:S(2)}) async-start(), calls=%async_computation.14 | async-start | bytes 4325376 | tf_op jit(solution)/shard_map/reduce_scatter | solution.py:353
  168.9 418.9 %reduce-scatter.24.cloned.1.call-start = ((), (), s32[]{:S(2)}) async-start(), calls=%async_computation.15 | async-start | bytes 4325376 | tf_op jit(solution)/shard_map/reduce_scatter | solution.py:354
  173.5 595.9 %reduce-scatter.14.cloned.1.call-start = ((), (), s32[]{:S(2)}) async-start(), calls=%async_computation.10 | async-start | bytes 17301504 | tf_op jit(solution)/shard_map/reduce_scatter | solution.py:348
  178.3 6.7 copy-start.7
  178.3 6.7 copy-start.43
  227.9 728.8 %reduce-scatter.10.cloned.1.call-start = ((), (), s32[]{:S(2)}) async-start(), calls=%async_computation.8 | async-start | bytes 17301504 | tf_op jit(solution)/shard_map/reduce_scatter | solution.py:346
  296.5 847.5 %reduce-scatter.16.cloned.1.call-start = ((), (), s32[]{:S(2)}) async-start(), calls=%async_computation.11 | async-start | bytes 17301504 | tf_op jit(solution)/shard_map/reduce_scatter | solution.py:349
  296.6 10.7 slice-start
  296.6 10.5 copy-start.9
  296.6 10.5 copy-start.20
  296.6 10.7 slice-start.1
  296.6 10.7 copy-start.34
  296.6 10.7 copy-start.46
  296.7 10.7 copy-start.48
  345.9 985.6 %reduce-scatter.20.cloned.1.call-start = ((), (), s32[]{:S(2)}) async-start(), calls=%async_computation.13 | async-start | bytes 17301504 | tf_op jit(solution)/shard_map/reduce_scatter | solution.py:351
  374.4 1229.9 %reduce-scatter.18.cloned.1.call-start = ((), (), s32[]{:S(2)}) async-start(), calls=%async_computation.12 | async-start | bytes 25952256 | tf_op jit(solution)/shard_map/reduce_scatter | solution.py:350
  406.8 1561.0 %reduce-scatter.12.cloned.1.call-start = ((), (), s32[]{:S(2)}) async-start(), calls=%async_computation.9 | async-start | bytes 34603008 | tf_op jit(solution)/shard_map/reduce_scatter | solution.py:347
  455.0 52.2 %copy-start.16 = (f32[1,304,512]{2,1,0:T(8,128)}, f32[1,304,512]{2,1,0:T(8,128)S(1)}, u32[]{:S(2)}) copy-start(f32[1,304,512]{2,1,0:T(8,128)S(1)} %reshape.558) | copy-start | bytes 1867780
  455.0 8.2 copy-start.32
  455.0 8.3 copy-start.30
  463.4 44.7 %copy-start.8 = (f32[1,288,512]{2,1,0:T(8,128)S(1)}, f32[1,288,512]{2,1,0:T(8,128)}, u32[]{:S(2)}) copy-start(f32[1,288,512]{2,1,0:T(8,128)} %copy-done.7) | copy-start | bytes 1769476
  463.4 44.7 %copy-start.44 = (f32[288]{0:T(512)S(1)}, f32[288]{0:T(512)}, u32[]{:S(2)}) copy-start(f32[288]{0:T(512)} %copy-done.43) | copy-start | bytes 3460
  463.5 44.6 %copy-start.18 = (f32[1,300,512]{2,1,0:T(8,128)S(1)}, f32[1,300,512]{2,1,0:T(8,128)}, u32[]{:S(2)}) copy-start(f32[1,300,512]{2,1,0:T(8,128)} %reshape.553) | copy-start | bytes 1843204
  508.3 1459.5 %copy-start.1 = (bf16[512,2048]{1,0:T(8,128)(2,1)S(1)}, bf16[512,2048]{1,0:T(8,128)(2,1)}, u32[]{:S(2)}) copy-start(bf16[512,2048]{1,0:T(8,128)(2,1)} %param.48) | copy-start | bytes 6291460
  (50 other events, 118.5 us)
Sparse Core Ops, SparseCore 0:
  164.2 137.3 all-reduce.49
  304.4 141.5 reduce-scatter.21
  448.9 138.8 reduce-scatter.23
  590.5 178.7 reduce-scatter.13
  772.0 184.5 reduce-scatter.9
  959.4 184.5 reduce-scatter.15
  1146.9 184.5 reduce-scatter.19
  1334.4 269.8 reduce-scatter.17
  1607.2 360.6 reduce-scatter.11
where the time goes:
time: 2000 us; the launch traced here: 1970 us
  waiting for transfers between devices  1460 us (73%)
  local copies, waits for them, and re-layouts  302 us (15%)
  matrix products  125 us (6%)
  blocking collectives  43.5 us (2%)
  other arithmetic  31.6 us (2%)
    reduce_scatter x1, waiting for transfers between devices, body(): lax.psum_scatter(fine_grads[2], 'dp', scatter_dimension=1, tiled=True)  364 us
    reduce_scatter x1, waiting for transfers between devices, body(): lax.psum_scatter(coarse_grads[2], 'dp', scatter_dimension=1, tiled=True)  273 us
    reduce_scatter x1, waiting for transfers between devices, body(): lax.psum_scatter(coarse_grads[4], 'dp', scatter_dimension=1, tiled=True)  188 us
    reduce_scatter x1, waiting for transfers between devices, body(): lax.psum_scatter(coarse_grads[0], 'dp', scatter_dimension=1, tiled=True)  187 us
    reduce_scatter x1, waiting for transfers between devices, body(): lax.psum_scatter(fine_grads[0], 'dp', scatter_dimension=1, tiled=True)  187 us
    reduce_scatter x1, waiting for transfers between devices, body(): lax.psum_scatter(fine_grads[4], 'dp', scatter_dimension=1, tiled=True)  182 us
    unnamed x162, local copies, waits for them, and re-layouts  111 us
    reduce_scatter x1, waiting for transfers between devices, body(): lax.psum_scatter(reduce_grad, 'dp', scatter_dimension=0, tiled=True)  76.3 us
  transfers between devices with their start and end apart: 9, of which 7 were waited for; matrix products, arithmetic and copies ran while one was open for 15% of the time, Pallas kernels for 0%

commit v1 on v0

v1 whole, which is shorter than its diff:
```python
from functools import partial

import jax
import jax.numpy as jnp
from jax import lax
from jax.experimental import pallas as pl
from jax.experimental.pallas import tpu as pltpu
from jax.sharding import PartitionSpec as P

K_A = 12
K_B = 16


EPSILON = 1e-05
HORIZON_ENDS = (192, 288, 432, 816)
FLOAT = jnp.float32
BFLOAT = jnp.bfloat16


def product(operand, matrix):
    return jnp.dot(operand, matrix, preferred_element_type=FLOAT)


def product_back(gradient, matrix):
    return lax.dot_general(gradient, matrix, (((1,), (1,)), ((), ())), preferred_element_type=FLOAT)


def valid_masks(horizon, length_total):
    valid_ends = jnp.zeros(horizon.shape, jnp.int32)
    for number, ending in enumerate(HORIZON_ENDS):
        valid_ends = valid_ends + jnp.where(horizon == number, length_total * ending, 0).astype(
            jnp.int32
        )
    positions = lax.iota(jnp.int32, length_total) * 816
    return (positions[None, :] < valid_ends[:, None]).astype(FLOAT)


def _pad8(count):
    return -(-count // 8)


def _assemble(weight_ref, wide_ref, taps, slab):
    rows = min(8, taps - 8 * slab)

    def step(number, carry):
        for inner in range(4):
            pair = number * 4 + inner
            start = pl.multiple_of(pair * 1024, 1024)
            values = weight_ref[8 * slab : 8 * slab + rows, pl.ds(start, 1024)].astype(FLOAT)
            if rows < 8:
                values = jnp.concatenate([values, jnp.zeros((8 - rows, 1024), FLOAT)], axis=0)
            both = jnp.concatenate([values[:, :512], values[:, 512:]], axis=0)
            first = pl.multiple_of(pair * 16, 16)
            wide_ref[pl.ds(first, 16), :] = both.astype(BFLOAT)
        return carry

    lax.fori_loop(0, 16, step, 0)


def _statistics(values):
    average = jnp.mean(values, axis=-1, keepdims=True)
    centered = values - average
    variance = jnp.mean(centered * centered, axis=-1, keepdims=True)
    scale = lax.rsqrt(variance + EPSILON)
    return centered * scale, scale


def _norm_back(grad, normalized, scale, gain):
    weighted = grad * gain
    first = jnp.mean(weighted, axis=-1, keepdims=True)
    second = jnp.mean(weighted * normalized, axis=-1, keepdims=True)
    return scale * (weighted - first - normalized * second)


def _lanes(values):
    return [values[:, 128 * block : 128 * (block + 1)] for block in range(4)]


def forward_kernel(
    kernel,
    steps,
    bias,
    series_ref,
    params_ref,
    down_ref,
    iso_ref,
    up_ref,
    low_ref,
    up_out_ref,
    season_ref,
    down_out_ref,
    iso_out_ref,
    joined_ref,
    columns_ref,
    edge_ref,
    spread_ref,
    order_ref,
    wide_ref,
    rows_ref,
    taps_ref,
    sum_ref,
    raised_ref,
):
    length = series_ref.shape[0]
    half = kernel // 2
    window = kernel + 1
    tap_slabs = _pad8(kernel)
    iso_slabs = _pad8(steps)
    number = pl.program_id(0)
    block = lax.rem(number, 4)

    def rearranged(pieces, slabs):
        ordered = jnp.dot(
            jnp.concatenate(pieces, axis=0), order_ref[...], preferred_element_type=FLOAT
        )
        rows_ref[0 : slabs * 128, :] = ordered.astype(BFLOAT)

    def contract(weight_ref, taps, slabs):
        total = sum_ref[...]
        for slab in range(slabs):
            _assemble(weight_ref, wide_ref, taps, slab)
            first = pl.multiple_of((slab * 4 + block) * 32, 32)
            total = total + jnp.dot(
                rows_ref[pl.ds(first, 32), :], wide_ref[...], preferred_element_type=FLOAT
            )
        sum_ref[...] = total

    @pl.when(number == 0)
    def _():
        source = lax.broadcasted_iota(jnp.int32, (1024, 1024), 0)
        target = lax.broadcasted_iota(jnp.int32, (1024, 1024), 1)
        wanted = (source & 127) * 8 + (source >> 7)
        order_ref[...] = jnp.where(target == wanted, 1.0, 0.0).astype(BFLOAT)
        edge_ref[16 : 16 + length, :] = series_ref[...].astype(FLOAT)
        edge_ref[0:16, :] = jnp.broadcast_to(edge_ref[16:17, :], (16, 512))
        edge_ref[16 + length : 32 + length, :] = jnp.broadcast_to(
            edge_ref[15 + length : 16 + length, :], (16, 512)
        )
        spread_ref[...] = jnp.zeros_like(spread_ref)
        for lane in range(4):
            columns = slice(128 * lane, 128 * (lane + 1))
            running = edge_ref[16 - half : 16 - half + length, columns]
            for offset in range(1, window):
                first = 16 - half + offset
                running = running + edge_ref[first : first + length, columns]
            season = edge_ref[16 : 16 + length, columns] - running / window
            season_ref[:, columns] = season
            spread_ref[lane, half : half + length, :] = season
        pieces = []
        for slab in range(tap_slabs):
            for lane in range(4):
                parts = []
                for tap in range(8 * slab, 8 * slab + 8):
                    if tap < kernel:
                        part = spread_ref[lane, pl.ds(tap, 32, stride=kernel), :]
                    else:
                        part = jnp.zeros((32, 128), FLOAT)
                    parts.append(part.astype(BFLOAT))
                pieces.append(jnp.concatenate(parts, axis=1))
        rearranged(pieces, tap_slabs)
        sum_ref[...] = jnp.zeros_like(sum_ref)
        for group in range(kernel // 4):
            for lane in range(4):
                stacked = jnp.concatenate(
                    [
                        spread_ref[lane, pl.ds(4 * group + inner, 32, stride=kernel), :]
                        for inner in range(4)
                    ],
                    axis=0,
                )
                columns_ref[
                    128 * lane : 128 * (lane + 1), 128 * group : 128 * (group + 1)
                ] = stacked.T.astype(BFLOAT)

    @pl.when(number < 4)
    def _():
        contract(down_ref, kernel, tap_slabs)

    @pl.when(number == 3)
    def _():
        down_out = jnp.tanh(sum_ref[...] + params_ref[bias + 0 : bias + 1, :])
        down_out_ref[...] = down_out
        edge_ref[0:32, :] = jnp.zeros((32, 512), FLOAT)
        edge_ref[32:64, :] = down_out
        place = lax.broadcasted_iota(jnp.int32, (128, 128), 0)
        for lane, values in enumerate(_lanes(down_out)):
            padded = jnp.concatenate([values, jnp.zeros((96, 128), FLOAT)], axis=0)
            columns_ref[128 * lane : 128 * (lane + 1), 32 * kernel :] = jnp.where(
                place < steps, padded, 0.0
            ).T.astype(BFLOAT)
        pieces = []
        for slab in range(iso_slabs):
            for lane in range(4):
                columns = slice(128 * lane, 128 * (lane + 1))
                parts = []
                for tap in range(8 * slab, 8 * slab + 8):
                    if tap < steps:
                        first = 33 - steps + tap
                        part = edge_ref[first : first + 32, columns]
                    else:
                        part = jnp.zeros((32, 128), FLOAT)
                    parts.append(part.astype(BFLOAT))
                pieces.append(jnp.concatenate(parts, axis=1))
        rearranged(pieces, iso_slabs)
        sum_ref[...] = jnp.zeros_like(sum_ref)

    @pl.when((number >= 4) & (number < 8))
    def _():
        contract(iso_ref, steps, iso_slabs)

    @pl.when(number == 7)
    def _():
        iso_out = jnp.tanh(sum_ref[...] + params_ref[bias + 1 : bias + 2, :])
        iso_out_ref[...] = iso_out
        normalized, _ = _statistics(iso_out + down_out_ref[...])
        keep = lax.broadcasted_iota(jnp.int32, (32, 512), 0) < steps
        joined = jnp.where(
            keep, normalized * params_ref[6:7, :] + params_ref[7:8, :], 0.0
        ).astype(BFLOAT)
        joined_ref[...] = joined
        stacked = jnp.concatenate(_lanes(joined), axis=0)
        for tap in range(8):
            ordered = jnp.dot(
                stacked,
                order_ref[128 * tap : 128 * (tap + 1), :],
                preferred_element_type=FLOAT,
            ).astype(BFLOAT)
            for lane in range(4):
                first = lane * 256 + tap * 32
                taps_ref[first : first + 32, :] = ordered[32 * lane : 32 * (lane + 1), :]
        raised_ref[...] = jnp.zeros_like(raised_ref)

    @pl.when(number >= 8)
    def _():
        for slab in range(tap_slabs):
            _assemble(up_ref, wide_ref, kernel, slab)
            raised_ref[slab * 256 : (slab + 1) * 256, :] += jnp.dot(
                taps_ref[pl.ds(pl.multiple_of(block * 256, 256), 256), :],
                wide_ref[...],
                preferred_element_type=FLOAT,
            )

    @pl.when(number == 11)
    def _():
        for tap in range(kernel):
            for lane in range(4):
                spread_ref[lane, pl.ds(tap, 32, stride=kernel), :] = raised_ref[
                    32 * tap : 32 * (tap + 1), 128 * lane : 128 * (lane + 1)
                ]

        def finish(chunk, carry):
            rows = pl.ds(pl.multiple_of(chunk * 32, 32), 32)
            raised = jnp.concatenate([spread_ref[lane, rows, :] for lane in range(4)], axis=1)
            up_out = jnp.tanh(raised + params_ref[bias + 2 : bias + 3, :])
            up_out_ref[rows, :] = up_out
            normalized, _ = _statistics(up_out + season_ref[rows, :])
            low_ref[rows, :] = (
                normalized * params_ref[6:7, :] + params_ref[7:8, :]
            ).astype(BFLOAT)
            return carry

        lax.fori_loop(0, length // 32, finish, 0)


def _product(wide_ref, right_ref, slab):
    return lax.dot_general(
        wide_ref[...],
        right_ref[slab * 256 : (slab + 1) * 256, :],
        (((1,), (1,)), ((), ())),
        preferred_element_type=FLOAT,
    )


def _diagonal(wide, wide_out_ref):
    for part in range(2):
        wide_out_ref[part] = wide[:, 128 * part : 128 * (part + 1)]
    lane = lax.broadcasted_iota(jnp.int32, (128, 128), 1) >> 5
    halves = []
    for part in range(2):
        total = jnp.zeros((128, 128), FLOAT)
        for inner in range(4):
            tap = part * 4 + inner
            rows = wide_out_ref[part, pl.ds(tap, 128, stride=8), :]
            total = jnp.where(lane == inner, rows, total)
        halves.append(total)
    return halves


def _split(values):
    first = values.astype(BFLOAT).astype(FLOAT)
    second = (values - first).astype(BFLOAT).astype(FLOAT)
    return first, second, values - first - second


def outer_kernel(
    devices,
    kernels,
    grad_ref,
    up_fine_ref,
    season_fine_ref,
    joined_fine_ref,
    up_coarse_ref,
    season_coarse_ref,
    joined_coarse_ref,
    params_ref,
    vectors_ref,
    send_ref,
    right_fine_ref,
    right_coarse_ref,
    outer_fine_ref,
    outer_coarse_ref,
    spread_ref,
    sums_ref,
):
    length = grad_ref.shape[0]
    gain = params_ref[6:7, :]
    empty = jnp.zeros((1, 512), FLOAT)
    known = vectors_ref.shape[0]
    sums_ref[0:known, :] = vectors_ref[...]
    sums_ref[known + 2 : known + 4, :] = jnp.zeros((2, 512), FLOAT)
    branches = (
        (up_fine_ref, season_fine_ref, right_fine_ref, outer_fine_ref),
        (up_coarse_ref, season_coarse_ref, right_coarse_ref, outer_coarse_ref),
    )
    for branch, (up_ref, season_ref, right_ref, outer_ref) in enumerate(branches):
        kernel = kernels[branch]
        columns = slice(512 * branch, 512 * (branch + 1))
        spread_ref[...] = jnp.zeros_like(spread_ref)

        def outer(chunk, carry):
            gain_sum, shift_sum, bias_sum = carry
            rows = pl.ds(pl.multiple_of(chunk * 32, 32), 32)
            grad = grad_ref[rows, columns]
            up_out = up_ref[rows, :]
            normalized, scale = _statistics(up_out + season_ref[rows, :])
            back = _norm_back(grad, normalized, scale, gain)
            outer_ref[rows, :] = back
            raised = (back * (1.0 - up_out * up_out)).astype(BFLOAT).astype(FLOAT)
            for lane, values in enumerate(_lanes(raised)):
                spread_ref[lane, rows, :] = values
            return (
                gain_sum + jnp.sum(grad * normalized, axis=0, keepdims=True),
                shift_sum + jnp.sum(grad, axis=0, keepdims=True),
                bias_sum + jnp.sum(raised, axis=0, keepdims=True),
            )

        gain_sum, shift_sum, bias_sum = lax.fori_loop(
            0, length // 32, outer, (empty, empty, empty)
        )
        sums_ref[known + branch : known + branch + 1, :] = bias_sum
        sums_ref[known + 2 : known + 3, :] += gain_sum
        sums_ref[known + 3 : known + 4, :] += shift_sum
        for tap in range(8 * _pad8(kernel)):
            rows = slice(32 * tap, 32 * (tap + 1))
            if tap < kernel:
                right_ref[rows, :] = jnp.concatenate(
                    [spread_ref[lane, pl.ds(tap, 32, stride=kernel), :] for lane in range(4)],
                    axis=1,
                ).astype(BFLOAT)
            else:
                right_ref[rows, :] = jnp.zeros((32, 512), BFLOAT)
    place = lax.broadcasted_iota(jnp.int32, (32, 512), 0)
    for target in range(devices):
        first = 64 * target
        block = slice(first + 32, first + 64)
        branch = 0 if target < kernels[0] else 1
        tap = target - branch * kernels[0]
        if tap < kernels[branch]:
            rows = branches[branch][2][32 * tap : 32 * (tap + 1), :]
            if target < known + 4:
                rows = rows.astype(FLOAT)
                for inner, part in enumerate(_split(sums_ref[target : target + 1, :])):
                    rows = jnp.where(place == 29 + inner, part, rows)
                rows = rows.astype(BFLOAT)
            send_ref[block, :] = rows
            send_ref[first : first + 32, :] = (joined_fine_ref, joined_coarse_ref)[branch][...]
        else:
            send_ref[first : first + 64, :] = jnp.zeros((64, 512), BFLOAT)


def inner_kernel(
    steps,
    slabs,
    right_in_ref,
    down_out_ref,
    iso_out_ref,
    params_ref,
    up_ref,
    iso_ref,
    pack_ref,
    grad_down_ref,
    sums_ref,
    rows_ref,
    wide_ref,
    right_ref,
    wide_out_ref,
    turned_ref,
    shift_ref,
    inner_ref,
):
    iso_slabs = _pad8(steps)
    number = pl.program_id(0)
    block = lax.rem(number, 4)
    gain = params_ref[6:7, :]

    def contract(weight_ref, taps, count, operand_ref):
        total = None
        for slab in range(count):
            _assemble(weight_ref, wide_ref, taps, slab)
            term = _product(wide_ref, operand_ref, slab)
            total = term if total is None else total + term
        first, second = _diagonal(total, wide_out_ref)
        folded = first + second
        folded = folded + pltpu.roll(folded, 64, 1)
        folded = folded + pltpu.roll(folded, 32, 1)
        turned_ref[pl.ds(pl.multiple_of(block * 128, 128), 128), :] = folded

    def collected():
        return turned_ref[...].T[0:32, :]

    @pl.when(number < 4)
    def _():
        contract(up_ref, up_ref.shape[0], slabs, right_in_ref)

    @pl.when(number == 3)
    def _():
        grad = collected()
        iso_out = iso_out_ref[...]
        normalized, scale = _statistics(iso_out + down_out_ref[...])
        back = _norm_back(grad, normalized, scale, gain)
        inner_ref[...] = back
        sums_ref[0:1, :] = jnp.sum(grad * normalized, axis=0, keepdims=True)
        sums_ref[1:2, :] = jnp.sum(grad, axis=0, keepdims=True)
        low = (back * (1.0 - iso_out * iso_out)).astype(BFLOAT)
        rows_ref[0:32, :] = low.astype(FLOAT)
        shift_ref[...] = jnp.zeros_like(shift_ref)
        shift_ref[32:64, :] = low.astype(FLOAT)
        for tap in range(8 * iso_slabs):
            if tap < steps:
                first = 31 + steps - tap
                values = shift_ref[first : first + 32, :].astype(BFLOAT)
            else:
                values = jnp.zeros((32, 512), BFLOAT)
            right_ref[32 * tap : 32 * (tap + 1), :] = values

    @pl.when(number >= 4)
    def _():
        contract(iso_ref, steps, iso_slabs, right_ref)

    @pl.when(number == 7)
    def _():
        down_out = down_out_ref[...]
        keep = lax.broadcasted_iota(jnp.int32, (32, 512), 0) < steps
        grad = jnp.where(keep, inner_ref[...] + collected(), 0.0)
        low = (grad * (1.0 - down_out * down_out)).astype(BFLOAT)
        grad_down_ref[...] = low
        rows_ref[32:64, :] = jnp.zeros((32, 512), FLOAT)
        rows_ref[steps : steps + 32, :] = low.astype(FLOAT)
        for item in range(2):
            high, middle, _ = _split(sums_ref[item : item + 1, :])
            first = 2 * steps + 2 * item
            rows_ref[first : first + 1, :] = high
            rows_ref[first + 1 : first + 2, :] = middle
        pack_ref[...] = rows_ref[0 : pack_ref.shape[0], :].astype(BFLOAT)


def series_kernel(
    kernels,
    grad_fine_ref,
    grad_coarse_ref,
    outer_fine_ref,
    outer_coarse_ref,
    fine_ref,
    coarse_ref,
    series_ref,
    spread_ref,
    wide_ref,
    right_ref,
    wide_out_ref,
    turned_ref,
):
    length = series_ref.shape[0]
    number = pl.program_id(0)
    block = lax.rem(number, 4)
    branches = (
        (grad_fine_ref, outer_fine_ref, fine_ref),
        (grad_coarse_ref, outer_coarse_ref, coarse_ref),
    )
    for branch, (grad_ref, outer_ref, weight_ref) in enumerate(branches):
        kernel = kernels[branch]
        half = kernel // 2
        window = kernel + 1

        @pl.when(number == 4 * branch)
        def _(grad_ref=grad_ref):
            for tap in range(8):
                right_ref[32 * tap : 32 * (tap + 1), :] = grad_ref[...]

        @pl.when((number >= 4 * branch) & (number < 4 * branch + 4))
        def _(weight_ref=weight_ref, kernel=kernel):
            for slab in range(_pad8(kernel)):
                _assemble(weight_ref, wide_ref, kernel, slab)
                halves = _diagonal(_product(wide_ref, right_ref, 0), wide_out_ref)
                rows = pl.ds(pl.multiple_of(block * 128, 128), 128)
                for part in range(2):
                    turned_ref[2 * slab + part, rows, :] = halves[part]

        @pl.when(number == 4 * branch + 3)
        def _(outer_ref=outer_ref, kernel=kernel, half=half, window=window, branch=branch):
            spread_ref[...] = jnp.zeros_like(spread_ref)
            for tap in range(kernel):
                lane0 = 32 * (tap % 4)
                if tap % 4 == 0:
                    turned = turned_ref[tap // 4].T
                for lane in range(4):
                    spread_ref[lane, pl.ds(tap, 32, stride=kernel), :] = turned[
                        lane0 : lane0 + 32, 128 * lane : 128 * (lane + 1)
                    ]
            for lane in range(4):
                columns = slice(128 * lane, 128 * (lane + 1))
                season = outer_ref[:, columns] + spread_ref[lane, half : half + length, :]
                spread_ref[lane, 0:24, :] = jnp.zeros((24, 128), FLOAT)
                spread_ref[lane, 24 : 24 + length, :] = season
                spread_ref[lane, 24 + length : 48 + length, :] = jnp.zeros((24, 128), FLOAT)
                running = spread_ref[lane, 24 - half : 24 - half + length, :]
                for offset in range(1, window):
                    first = 24 - half + offset
                    running = running + spread_ref[lane, first : first + length, :]
                row = lax.broadcasted_iota(jnp.int32, (16, 128), 0)
                head = jnp.maximum(half + 1 - row, 0).astype(FLOAT)
                tail = jnp.maximum(row + half - 14, 0).astype(FLOAT)
                top = jnp.sum(season[0:16, :] * head, axis=0, keepdims=True)
                bottom = jnp.sum(season[length - 16 :, :] * tail, axis=0, keepdims=True)
                place = lax.broadcasted_iota(jnp.int32, (length, 128), 0)
                running = jnp.where(place == 0, top, running)
                running = jnp.where(place == length - 1, bottom, running)
                result = season - running / window
                if branch > 0:
                    result = result + series_ref[:, columns]
                series_ref[:, columns] = result


def _blocks(start):
    def index(number):
        return (0, jnp.clip(number - start, 0, 3))

    return index


def _whole(shape):
    return pl.BlockSpec(shape, lambda number: (0,) * len(shape))


def forward_branch(series, params, weights, kernel, steps, bias):
    down, iso, up = weights
    length = series.shape[0]
    width = 128 * 512
    shapes = [
        jax.ShapeDtypeStruct((length, 512), BFLOAT),
        jax.ShapeDtypeStruct((length, 512), FLOAT),
        jax.ShapeDtypeStruct((length, 512), FLOAT),
        jax.ShapeDtypeStruct((32, 512), FLOAT),
        jax.ShapeDtypeStruct((32, 512), FLOAT),
        jax.ShapeDtypeStruct((32, 512), BFLOAT),
        jax.ShapeDtypeStruct((512, 32 * kernel + 128), BFLOAT),
    ]
    return pl.pallas_call(
        partial(forward_kernel, kernel, steps, bias),
        grid=(12,),
        in_specs=[
            _whole((length, 512)),
            _whole(params.shape),
            pl.BlockSpec((kernel, width), _blocks(0)),
            pl.BlockSpec((steps, width), _blocks(4)),
            pl.BlockSpec((kernel, width), _blocks(8)),
        ],
        out_specs=[_whole(item.shape) for item in shapes],
        out_shape=shapes,
        scratch_shapes=[
            pltpu.VMEM((length + 32, 512), FLOAT),
            pltpu.VMEM((4, 512, 128), FLOAT),
            pltpu.VMEM((1024, 1024), BFLOAT),
            pltpu.VMEM((1024, 512), BFLOAT),
            pltpu.VMEM((512, 1024), BFLOAT),
            pltpu.VMEM((1024, 1024), BFLOAT),
            pltpu.VMEM((32, 512), FLOAT),
            pltpu.VMEM((512, 512), FLOAT),
        ],
        cost_estimate=_cost(90e6),
    )(series, params, down, iso, up)


def outer_grads(grad, fine_saved, coarse_saved, params, vectors, devices):
    length = grad.shape[0]
    kernels = (K_A, K_B)
    shapes = [
        jax.ShapeDtypeStruct((devices * 64, 512), BFLOAT),
        jax.ShapeDtypeStruct((256 * _pad8(K_A), 512), BFLOAT),
        jax.ShapeDtypeStruct((256 * _pad8(K_B), 512), BFLOAT),
        jax.ShapeDtypeStruct((length, 512), FLOAT),
        jax.ShapeDtypeStruct((length, 512), FLOAT),
    ]
    return pl.pallas_call(
        partial(outer_kernel, devices, kernels),
        out_shape=shapes,
        scratch_shapes=[pltpu.VMEM((4, 512, 128), FLOAT), pltpu.VMEM((16, 512), FLOAT)],
        cost_estimate=_cost(1e5),
    )(
        grad,
        fine_saved[1],
        fine_saved[2],
        fine_saved[5],
        coarse_saved[1],
        coarse_saved[2],
        coarse_saved[5],
        params,
        vectors,
    )


def _cost(read):
    return pl.CostEstimate(flops=0, bytes_accessed=int(read), transcendentals=0)


def inner_grads(right, saved, params, iso, up):
    kernel, steps = up.shape[0], iso.shape[0]
    width = 128 * 512
    shapes = [
        jax.ShapeDtypeStruct((8 * _pad8(2 * steps + 4), 512), BFLOAT),
        jax.ShapeDtypeStruct((32, 512), BFLOAT),
    ]
    return pl.pallas_call(
        partial(inner_kernel, steps, _pad8(kernel)),
        grid=(8,),
        in_specs=[
            _whole(right.shape),
            _whole((32, 512)),
            _whole((32, 512)),
            _whole(params.shape),
            pl.BlockSpec((kernel, width), _blocks(0)),
            pl.BlockSpec((steps, width), _blocks(4)),
        ],
        out_specs=[_whole(item.shape) for item in shapes],
        out_shape=shapes,
        scratch_shapes=[
            pltpu.VMEM((8, 512), FLOAT),
            pltpu.VMEM((64, 512), FLOAT),
            pltpu.VMEM((1024, 512), BFLOAT),
            pltpu.VMEM((1024, 512), BFLOAT),
            pltpu.VMEM((2, 1024, 128), FLOAT),
            pltpu.VMEM((512, 128), FLOAT),
            pltpu.VMEM((96, 512), FLOAT),
            pltpu.VMEM((32, 512), FLOAT),
        ],
        cost_estimate=_cost(80e6),
    )(right, saved[3], saved[4], params, up, iso)


def series_grads(grads, outers, weights):
    length = outers[0].shape[0]
    width = 128 * 512
    shape = jax.ShapeDtypeStruct((length, 512), FLOAT)
    return pl.pallas_call(
        partial(series_kernel, (K_A, K_B)),
        grid=(8,),
        in_specs=[
            _whole((32, 512)),
            _whole((32, 512)),
            _whole((length, 512)),
            _whole((length, 512)),
            pl.BlockSpec((K_A, width), _blocks(0)),
            pl.BlockSpec((K_B, width), _blocks(4)),
        ],
        out_specs=_whole((length, 512)),
        out_shape=shape,
        scratch_shapes=[
            pltpu.VMEM((4, 512, 128), FLOAT),
            pltpu.VMEM((1024, 512), BFLOAT),
            pltpu.VMEM((256, 512), BFLOAT),
            pltpu.VMEM((2, 1024, 128), FLOAT),
            pltpu.VMEM((4, 512, 128), FLOAT),
        ],
        cost_estimate=_cost(80e6),
    )(grads[0], grads[1], outers[0], outers[1], weights[0], weights[1])


def _left_product(left, right):
    return lax.dot_general(left, right, (((0,), (0,)), ((), ())), preferred_element_type=FLOAT)


def table_kernel(*refs):
    table_ref = refs[-1]
    table_ref[...] = jnp.zeros_like(table_ref)
    row = 0
    for ref in refs[:-1]:
        values = ref[...].astype(FLOAT)
        for start in range(0, values.shape[0], 512):
            table_ref[row, :] = values[start : start + 512]
            row += 1


def vector_table(vectors):
    rows = sum(item.shape[0] for item in vectors) // 512
    return pl.pallas_call(
        table_kernel,
        out_shape=jax.ShapeDtypeStruct((8 * _pad8(rows), 512), FLOAT),
        cost_estimate=_cost(1e6),
    )(*vectors)


def dense_kernel(
    devices,
    fine_ref,
    coarse_ref,
    merge_ref,
    expand_ref,
    reduce_ref,
    params_ref,
    mask_ref,
    cotangent_ref,
    result_ref,
    branches_ref,
    rows_ref,
    sums_ref,
    merged_ref,
    normed_ref,
    wide_ref,
    active_ref,
    slope_ref,
    residual_ref,
    low_ref,
):
    length = fine_ref.shape[0]
    hidden = expand_ref.shape[1]
    merge_bias, first_gain, first_bias = [
        params_ref[item : item + 1, :] for item in range(8, 11)
    ]
    reduce_bias, final_gain, final_bias = [
        params_ref[item : item + 1, :] for item in range(11, 14)
    ]
    empty = jnp.zeros((1, 512), FLOAT)

    def chunks(step, carry):
        def run(chunk, carry):
            return step(pl.ds(pl.multiple_of(chunk * 32, 32), 32), carry)

        return lax.fori_loop(0, length // 32, run, carry)

    def total(values):
        return jnp.sum(values, axis=0, keepdims=True)

    own = 512 // devices
    shard = hidden // devices
    firsts = scatter_rows(devices, 512, hidden)

    def place(values, start, size, offset):
        values = values.astype(BFLOAT)
        for item in range(512 // size):
            row = firsts[start // size + item] + offset
            rows_ref[row : row + size, :] = values[item * size : (item + 1) * size, :]

    merged_ref[...] = (
        product(fine_ref[...], merge_ref[0:512, :])
        + product(coarse_ref[...], merge_ref[512:1024, :])
        + merge_bias
    )

    def first(rows, carry):
        normalized, _ = _statistics(merged_ref[rows, :])
        normed_ref[rows, :] = (normalized * first_gain + first_bias).astype(BFLOAT)
        return carry

    chunks(first, 0)
    for start in range(0, hidden, 512):
        columns = slice(start, start + 512)
        wide_ref[...] = product(normed_ref[...], expand_ref[:, columns])
        number = 14 + start // 512
        bias = params_ref[number : number + 1, :]

        def gate(rows, carry):
            values = wide_ref[rows, :] + bias
            chance = 0.5 + 0.5 * lax.erf(values * 0.7071067811865476)
            active_ref[rows, columns] = (values * chance).astype(BFLOAT)
            density = jnp.exp(-0.5 * values * values) * 0.3989422804014327
            slope_ref[rows, columns] = chance + values * density
            return carry

        chunks(gate, 0)
    wide_ref[...] = product(active_ref[...], reduce_ref[...])

    def final(rows, carry):
        bias_sum, gain_sum, shift_sum = carry
        normalized, scale = _statistics(merged_ref[rows, :] + (wide_ref[rows, :] + reduce_bias))
        mask = mask_ref[rows, :]
        result_ref[rows, :] = (normalized * final_gain + final_bias) * mask
        grad = cotangent_ref[rows, :].astype(FLOAT) * mask
        back = _norm_back(grad, normalized, scale, final_gain)
        residual_ref[rows, :] = back
        low = back.astype(BFLOAT)
        low_ref[rows, :] = low
        return (
            bias_sum + total(low.astype(FLOAT)),
            gain_sum + total(grad * normalized),
            shift_sum + total(grad),
        )

    bias_sum, gain_sum, shift_sum = chunks(final, (empty, empty, empty))
    sums_ref[3:4, :] = bias_sum
    sums_ref[4:5, :] = gain_sum
    sums_ref[5:6, :] = shift_sum
    for start in range(0, hidden, 512):
        columns = slice(start, start + 512)
        place(_left_product(active_ref[:, columns], low_ref[...]), start, shard, 2 * own + shard)
        wide_ref[...] = product_back(low_ref[...], reduce_ref[columns, :])

        def gate_back(rows, carry):
            low = (wide_ref[rows, :] * slope_ref[rows, columns]).astype(BFLOAT)
            active_ref[rows, columns] = low
            return carry + total(low.astype(FLOAT))

        number = 6 + start // 512
        sums_ref[number : number + 1, :] = chunks(gate_back, empty)
        place(_left_product(active_ref[:, columns], normed_ref[...]), start, shard, 2 * own)
    wide_ref[...] = product_back(active_ref[...], expand_ref[...])

    def first_back(rows, carry):
        bias_sum, gain_sum, shift_sum = carry
        normalized, scale = _statistics(merged_ref[rows, :])
        grad = wide_ref[rows, :]
        back = _norm_back(grad, normalized, scale, first_gain)
        low = (residual_ref[rows, :] + back).astype(BFLOAT)
        low_ref[rows, :] = low
        return (
            bias_sum + total(low.astype(FLOAT)),
            gain_sum + total(grad * normalized),
            shift_sum + total(grad),
        )

    bias_sum, gain_sum, shift_sum = chunks(first_back, (empty, empty, empty))
    sums_ref[0:1, :] = bias_sum
    sums_ref[1:2, :] = gain_sum
    sums_ref[2:3, :] = shift_sum
    for branch, low_in_ref in enumerate((fine_ref, coarse_ref)):
        columns = slice(512 * branch, 512 * (branch + 1))
        place(_left_product(low_in_ref[...], low_ref[...]), 0, own, branch * own)
        branches_ref[:, columns] = product_back(low_ref[...], merge_ref[columns, :])


def dense_block(devices, fine, coarse, merge, expand, reduce, params, mask, cotangent):
    length, channels = fine.shape
    hidden = expand.shape[1]
    known = 6 + hidden // channels
    shapes = [
        jax.ShapeDtypeStruct((length, channels), FLOAT),
        jax.ShapeDtypeStruct((length, 2 * channels), FLOAT),
        jax.ShapeDtypeStruct((2 * channels + 2 * hidden, channels), BFLOAT),
        jax.ShapeDtypeStruct((known, channels), FLOAT),
    ]
    return pl.pallas_call(
        partial(dense_kernel, devices),
        out_shape=shapes,
        scratch_shapes=[
            pltpu.VMEM((length, channels), FLOAT),
            pltpu.VMEM((length, channels), BFLOAT),
            pltpu.VMEM((length, channels), FLOAT),
            pltpu.VMEM((length, hidden), BFLOAT),
            pltpu.VMEM((length, hidden), FLOAT),
            pltpu.VMEM((length, channels), FLOAT),
            pltpu.VMEM((length, channels), BFLOAT),
        ],
        cost_estimate=_cost(70e6),
    )(fine, coarse, merge, expand, reduce, params, mask, cotangent)


def scatter_groups(devices):
    near = 8
    far = devices // near
    inside = [[first * near + item for item in range(near)] for first in range(far)]
    across = [[first * near + item for first in range(far)] for item in range(near)]
    return (inside, across)


def scatter_rows(devices, channels, hidden):
    own = channels // devices
    count = 2 * own + 2 * (hidden // devices)
    far = devices // 8
    return [((item % 8) * far + item // 8) * count for item in range(devices)]


def feed_part(rows, own):
    inside, _ = scatter_groups(rows.shape[1] // own)
    return lax.psum_scatter(
        rows, "dp", scatter_dimension=0, axis_index_groups=inside, tiled=True
    )


def feed_sums(part, own, hidden):
    channels = part.shape[1]
    _, across = scatter_groups(channels // own)
    pieces = lax.all_to_all(
        part.reshape(len(across[0]), -1, channels), "dp", 0, 0, axis_index_groups=across
    )
    summed = jnp.sum(pieces.astype(FLOAT), axis=0)
    first = 2 * own
    second = first + hidden
    return (
        summed[:first].reshape(2, own * channels),
        summed[first:second].T,
        summed[second:],
    )


def idle_kernel(*refs):
    del refs


def after(values, other):
    anywhere = pl.BlockSpec(memory_space=pl.ANY)
    return pl.pallas_call(
        idle_kernel,
        out_shape=jax.ShapeDtypeStruct(values.shape, values.dtype),
        in_specs=[anywhere, anywhere],
        out_specs=anywhere,
        input_output_aliases={0: 0},
        cost_estimate=_cost(1e5),
    )(values, other)


def exchange(values):
    return lax.all_to_all(values, "dp", 0, 0, tiled=False)


def weight_kernel(kernel, steps, offset, first, ups, columns_ref, grads_ref, *refs):
    blocks_ref = refs[0] if ups else None
    refs = refs[1:] if ups else refs
    down_ref, iso_ref, sums_ref = refs[:3]
    up_refs = refs[3 : 3 + ups]
    left_ref, right_ref, turned_ref, spread_ref = refs[3 + ups :]
    devices, own = columns_ref.shape[:2]
    width = devices * 32
    lane = lax.broadcasted_iota(jnp.int32, (own, 128), 1) >> 5
    for group in range(devices // 4):
        lanes = slice(128 * group, 128 * (group + 1))
        for piece in range(kernel // 4 + 1):
            start = offset + 128 * piece
            parts = [
                columns_ref[4 * group + item, :, start : start + 128].astype(FLOAT)
                for item in range(4)
            ]
            for inner in range(4 if piece < kernel // 4 else 1):
                total = parts[inner]
                for item in range(4):
                    if item != inner:
                        moved = pltpu.roll(parts[item], (32 * (item - inner)) % 128, 1)
                        total = jnp.where(lane == item, moved, total)
                if piece < kernel // 4:
                    tap = 4 * piece + inner
                    left_ref[own * tap : own * (tap + 1), lanes] = total.astype(BFLOAT)
                else:
                    turned_ref[:, lanes] = total
    place = lax.broadcasted_iota(jnp.int32, (own, width), 1) & 31
    ones = jnp.where(place < steps, 1.0, 0.0).astype(BFLOAT)

    def load(which):
        start = first + which * steps
        for item in range(devices):
            values = grads_ref[item, start : start + steps, :].astype(FLOAT)
            values = jnp.concatenate([values, jnp.zeros((32 - steps, 512), FLOAT)], axis=0)
            right_ref[32 * item : 32 * (item + 1), :] = values.astype(BFLOAT)

    def rows_out(values, out_ref, taps):
        for block, item in enumerate(_lanes(values)):
            spread_ref[block, 0 : values.shape[0], :] = item
        for channel in range(own):
            for block in range(4):
                start = 512 * channel + 128 * block
                out_ref[:, start : start + 128] = spread_ref[
                    block, pl.ds(channel, taps, stride=own), :
                ]

    load(1)
    left_ref[own * kernel : own * (kernel + 1), :] = ones
    values = product(left_ref[0 : own * (kernel + 1), :], right_ref[...])
    sums_ref[0:1, :] = values[own * kernel : own * kernel + 1, :]
    rows_out(values, down_ref, kernel)
    load(0)
    values = turned_ref[...]
    for tap in range(steps):
        shift = steps - 1 - tap
        moved = pltpu.roll(values, shift, 1) if shift else values
        moved = jnp.where((place >= shift) & (place < steps), moved, 0.0)
        left_ref[own * tap : own * (tap + 1), :] = moved.astype(BFLOAT)
    left_ref[own * steps : own * (steps + 1), :] = ones
    values = product(left_ref[0 : own * (steps + 1), :], right_ref[...])
    sums_ref[1:2, :] = values[own * steps : own * steps + 1, :]
    rows_out(values, iso_ref, steps)
    taps_before = 0
    for up_ref in up_refs:
        taps = up_ref.shape[0]
        values = blocks_ref[taps_before : taps_before + taps, 0:own, :].astype(FLOAT)
        rows_out(values.reshape(taps * own, 512), up_ref, taps)
        taps_before += taps


def weight_grads(columns, grads, blocks, kernel, steps, offset, first):
    devices, own = columns.shape[:2]
    channels = grads.shape[2]
    taps_up = () if blocks is None else (K_A, K_B)
    if own % 16 or devices % 4:
        iso_rows = grads[:, first : first + steps]
        down_rows = grads[:, first + steps : first + 2 * steps]
        down, iso = branch_products(
            columns[:, :, offset : offset + 32 * kernel + 128], iso_rows, down_rows, kernel
        )
        sums = [jnp.sum(item, axis=(0, 1), dtype=FLOAT) for item in (down_rows, iso_rows)]
        ups = []
        taps_before = 0
        for taps in taps_up:
            part = blocks[taps_before : taps_before + taps, :own].astype(FLOAT)
            ups.append(part.reshape(taps, own * channels))
            taps_before += taps
        return (down, iso, jnp.stack(sums, axis=0), *ups)
    shapes = [
        jax.ShapeDtypeStruct((kernel, own * channels), FLOAT),
        jax.ShapeDtypeStruct((steps, own * channels), FLOAT),
        jax.ShapeDtypeStruct((2, channels), FLOAT),
    ] + [jax.ShapeDtypeStruct((taps, own * channels), FLOAT) for taps in taps_up]
    highest = own * (max(kernel, steps) + 1)
    return pl.pallas_call(
        partial(weight_kernel, kernel, steps, offset, first, len(taps_up)),
        out_shape=shapes,
        scratch_shapes=[
            pltpu.VMEM((highest, devices * 32), BFLOAT),
            pltpu.VMEM((devices * 32, channels), BFLOAT),
            pltpu.VMEM((own, devices * 32), FLOAT),
            pltpu.VMEM((4, highest, 128), FLOAT),
        ],
        cost_estimate=_cost(17e6),
    )(columns, grads, *(() if blocks is None else (blocks,)))


def branch_products(columns, grad_iso, grad_down, kernel):
    devices, own = columns.shape[:2]
    steps, channels = grad_iso.shape[1:]
    patches = columns[:, :, : 32 * kernel].reshape(devices, own, kernel, 32)[..., :steps]
    down = jnp.einsum("nats,nsb->tab", patches, grad_down, preferred_element_type=FLOAT)
    mine = columns[:, :, 32 * kernel : 32 * kernel + steps]
    shifted = jnp.pad(mine, ((0, 0), (0, 0), (steps - 1, 0)))
    taps = jnp.stack([shifted[:, :, j : j + steps] for j in range(steps)], axis=0)
    iso = jnp.einsum("jnas,nsb->jab", taps, grad_iso, preferred_element_type=FLOAT)
    return (down.reshape(kernel, own * channels), iso.reshape(steps, own * channels))


def body(
    series,
    horizon,
    cotangent,
    fine_down,
    fine_down_bias,
    fine_isometric,
    fine_isometric_bias,
    fine_upsample,
    fine_upsample_bias,
    coarse_down,
    coarse_down_bias,
    coarse_isometric,
    coarse_isometric_bias,
    coarse_upsample,
    coarse_upsample_bias,
    branch_gain,
    branch_bias,
    merge_weight,
    merge_bias,
    first_gain,
    first_bias,
    expand_weight,
    expand_bias,
    reduce_weight,
    reduce_bias,
    final_gain,
    final_bias,
):
    batch_count, length_total, channels = series.shape
    row_count = batch_count * length_total
    devices = lax.axis_size("dp")
    own = channels // devices
    mask_rows = valid_masks(horizon, length_total).reshape(row_count, 1)
    steps = (fine_isometric.shape[0], coarse_isometric.shape[0])
    table = vector_table(
        [
            fine_down_bias,
            fine_isometric_bias,
            fine_upsample_bias,
            coarse_down_bias,
            coarse_isometric_bias,
            coarse_upsample_bias,
            branch_gain,
            branch_bias,
            merge_bias,
            first_gain,
            first_bias,
            reduce_bias,
            final_gain,
            final_bias,
            expand_bias,
        ]
    )
    fine_weights = (fine_down, fine_isometric, fine_upsample)
    coarse_weights = (coarse_down, coarse_isometric, coarse_upsample)
    rows_in = series.reshape(row_count, channels)
    fine_saved = forward_branch(rows_in, table, fine_weights, K_A, steps[0], 0)
    coarse_saved = forward_branch(rows_in, table, coarse_weights, K_B, steps[1], 3)
    columns_fine = exchange(fine_saved[6].reshape(devices, own, -1))
    columns_coarse = exchange(coarse_saved[6].reshape(devices, own, -1))
    merge_matrix = merge_weight.reshape(2 * channels, channels)
    result, grad_branches, dense_rows, vectors = dense_block(
        devices,
        after(fine_saved[0], columns_fine),
        coarse_saved[0],
        merge_matrix,
        expand_weight,
        reduce_weight,
        table,
        mask_rows,
        cotangent.reshape(row_count, channels),
    )
    result = result.reshape(batch_count, length_total, channels)
    known = vectors.shape[0]
    send, right_fine, right_coarse, outer_fine, outer_coarse = outer_grads(
        after(grad_branches, columns_coarse), fine_saved, coarse_saved, table, vectors, devices
    )
    received = exchange(send.reshape(devices, 64, channels))
    part = feed_part(after(dense_rows, send), own)
    pack_fine, down_fine = inner_grads(
        right_fine, fine_saved, table, fine_isometric, fine_upsample
    )
    pack_coarse, down_coarse = inner_grads(
        right_coarse, coarse_saved, table, coarse_isometric, coarse_upsample
    )
    packs = jnp.concatenate([pack_fine, pack_coarse], axis=0)
    packs = after(packs, received)
    down_coarse = after(down_coarse, packs)
    grads = lax.all_gather(packs, "dp", axis=0, tiled=False)
    second = pack_fine.shape[0]
    tap_product = jnp.einsum(
        "nsa,nsb->ab", received[:, :32], received[:, 32:], preferred_element_type=FLOAT
    )
    vector_sum = jnp.sum(received[:, 61:64].astype(FLOAT), axis=(0, 1)).reshape(1, channels)
    high = lax.reduce_precision(vector_sum, 8, 7)
    pair = jnp.concatenate([high, vector_sum - high], axis=0).astype(BFLOAT)
    blocks = jnp.concatenate(
        [
            tap_product.astype(BFLOAT).reshape(devices, own, channels),
            jnp.broadcast_to(pair[None], (devices, 2, channels)),
        ],
        axis=1,
    )
    blocks = exchange(blocks)
    series_gradient = series_grads(
        (down_fine, down_coarse), (outer_fine, outer_coarse), (fine_down, coarse_down)
    )
    part = after(part, series_gradient)
    dense = feed_sums(part, own, expand_weight.shape[1] // devices)
    series_gradient = series_gradient.reshape(series.shape)
    fine_down_gradient, fine_isometric_gradient, fine_sums = weight_grads(
        columns_fine, grads, None, K_A, steps[0], 0, 0
    )
    (
        coarse_down_gradient,
        coarse_isometric_gradient,
        coarse_sums,
        fine_upsample_gradient,
        coarse_upsample_gradient,
    ) = weight_grads(columns_coarse, grads, blocks, K_B, steps[1], 0, second)
    fine_down_bias_gradient, fine_isometric_bias_gradient = fine_sums[0], fine_sums[1]
    coarse_down_bias_gradient, coarse_isometric_bias_gradient = coarse_sums[0], coarse_sums[1]
    inner_sums = jnp.sum(
        grads[:, 2 * steps[0] : 2 * steps[0] + 4].astype(FLOAT)
        + grads[:, second + 2 * steps[1] : second + 2 * steps[1] + 4].astype(FLOAT),
        axis=0,
    )
    inner_sums = jnp.sum(inner_sums.reshape(2, 2, channels), axis=1)
    totals = jnp.sum(blocks[: known + 4, own:].astype(FLOAT), axis=1)
    merge_bias_gradient = totals[0]
    first_gain_gradient = totals[1]
    first_bias_gradient = totals[2]
    reduce_bias_gradient = totals[3]
    final_gain_gradient = totals[4]
    final_bias_gradient = totals[5]
    expand_bias_gradient = totals[6:known].reshape(-1)
    fine_upsample_bias_gradient = totals[known]
    coarse_upsample_bias_gradient = totals[known + 1]
    branch_gain_gradient = totals[known + 2] + inner_sums[0]
    branch_bias_gradient = totals[known + 3] + inner_sums[1]
    merge_weight_gradient, expand_weight_gradient, reduce_weight_gradient = dense
    return (
        result,
        series_gradient,
        fine_down_gradient,
        fine_down_bias_gradient,
        fine_isometric_gradient,
        fine_isometric_bias_gradient,
        fine_upsample_gradient,
        fine_upsample_bias_gradient,
        coarse_down_gradient,
        coarse_down_bias_gradient,
        coarse_isometric_gradient,
        coarse_isometric_bias_gradient,
        coarse_upsample_gradient,
        coarse_upsample_bias_gradient,
        branch_gain_gradient,
        branch_bias_gradient,
        merge_weight_gradient,
        merge_bias_gradient,
        first_gain_gradient,
        first_bias_gradient,
        expand_weight_gradient,
        expand_bias_gradient,
        reduce_weight_gradient,
        reduce_bias_gradient,
        final_gain_gradient,
        final_bias_gradient,
    )


def solution(mesh):
    in_specs = (
        P("dp", None, None),
        P("dp"),
        P("dp", None, None),
        P(),
        P(),
        P(),
        P(),
        P(),
        P(),
        P(),
        P(),
        P(),
        P(),
        P(),
        P(),
        P(),
        P(),
        P(),
        P(),
        P(),
        P(),
        P(),
        P(),
        P(),
        P(),
        P(),
        P(),
    )
    out_specs = (
        P("dp", None, None),
        P("dp", None, None),
        P(None, "dp"),
        P(),
        P(None, "dp"),
        P(),
        P(None, "dp"),
        P(),
        P(None, "dp"),
        P(),
        P(None, "dp"),
        P(),
        P(None, "dp"),
        P(),
        P(),
        P(),
        P(None, "dp"),
        P(),
        P(),
        P(),
        P(None, "dp"),
        P(),
        P("dp", None),
        P(),
        P(),
        P(),
    )
    return jax.shard_map(body, mesh=mesh, in_specs=in_specs, out_specs=out_specs, check_vma=False)
```

time: 2000 us -> 263 us (0.13); the launches traced: 1970 us -> 261 us
  waiting for transfers between devices: 1460 us -> 29.3 us
  local copies, waits for them, and re-layouts: 302 us -> 8.92 us
  Pallas kernels: 0 us -> 169 us
  matrix products: 125 us -> 2.28 us
  blocking collectives: 43.5 us -> 0 us
  starting transfers between devices: 0.37 us -> 29 us
  other arithmetic: 31.6 us -> 6.3 us
    reduce_scatter x8 -> x1, waiting for transfers between devices: 1460 us -> 0.01 us  [feed_part(): lax.psum_scatter(rows, 'dp', scatter_dimension=0, axis_index_groups=insid...]
    pallas_call x0 -> x16, Pallas kernels: none -> 169 us  [the longest x2 57.1 us: forward_branch(): pl.pallas_call(partial(forward_kernel, kernel, steps, bias), grid=(12,),...]
    reshape x23 -> x2, local copies, waits for them, and re-layouts: 145 us -> 0.71 us  [the longest x1 0.69 us: feed_sums(): summed[:first].reshape(2, own * channels)]
    dot_general x27 -> x1, matrix products: 125 us -> 2.28 us  [body(): jnp.einsum('nsa,nsb->ab', received[:, :32], received[:, 32:], preferred_e...]
    unnamed x162 -> x14, local copies, waits for them, and re-layouts: 111 us -> 2.83 us
    psum x1 -> x0, blocking collectives: 43.5 us -> none  [body(): lax.psum((fine_grads[1], fine_grads[3], fine_grads[5], coarse_grads[1], c...]
    all_to_all x0 -> x5, starting transfers between devices: none -> 28.5 us  [the longest x4 24.7 us: exchange(): return lax.all_to_all(values, 'dp', 0, 0, tiled=False)]
    all_to_all x0 -> x5, waiting for transfers between devices: none -> 25.5 us  [the longest x1 24.2 us: feed_sums(): lax.all_to_all(part.reshape(len(across[0]), -1, channels), 'dp', 0, 0, ax...]
  transfers between devices with their start and end apart: 9 -> 7, of which waited for: 7 -> 4; matrix products, arithmetic and copies ran while one was open for 15% -> 4% of each run, Pallas kernels for 0% -> 46%
where the time goes in v1:
time: 263 us; the launch traced here: 261 us
  Pallas kernels  169 us (64%)
  waiting for transfers between devices  29.3 us (11%)
  starting transfers between devices  29 us (11%)
  between operations  16.3 us (6%)
  local copies, waits for them, and re-layouts  8.92 us (3%)
  other arithmetic  6.3 us (2%)
    pallas_call x2, Pallas kernels, forward_branch(): pl.pallas_call(partial(forward_kernel, kernel, steps, bias), grid=(12,),...  57.1 us
    pallas_call x2, Pallas kernels, inner_grads(): pl.pallas_call(partial(inner_kernel, steps, _pad8(kernel)), grid=(8,), in...  46.9 us
    all_to_all x4, starting transfers between devices, exchange(): return lax.all_to_all(values, 'dp', 0, 0, tiled=False)  24.7 us
    all_to_all x1, waiting for transfers between devices, feed_sums(): lax.all_to_all(part.reshape(len(across[0]), -1, channels), 'dp', 0, 0, ax...  24.2 us
    pallas_call x1, Pallas kernels, dense_block(): pl.pallas_call(partial(dense_kernel, devices), out_shape=shapes, scratch_...  22.5 us
    pallas_call x1, Pallas kernels, series_grads(): pl.pallas_call(partial(series_kernel, (K_A, K_B)), grid=(8,), in_specs=[_...  21.6 us
    pallas_call x2, Pallas kernels, weight_grads(): pl.pallas_call(partial(weight_kernel, kernel, steps, offset, first, len(t...  10.4 us
    pallas_call x1, Pallas kernels, outer_grads(): pl.pallas_call(partial(outer_kernel, devices, kernels), out_shape=shapes,...  9.29 us
  transfers between devices with their start and end apart: 7, of which 4 were waited for; matrix products, arithmetic and copies ran while one was open for 4% of the time, Pallas kernels for 46%

profile of v1, /device:TPU:0, one launch (start us, length us, event | category | flops | bytes accessed | tf_op | source)
XLA Modules:
  0.0 261.4 jit_solution(4074611996432610171)
XLA Ops:
  8.0 1.5 shard_map.458.params_ref
  9.5 29.2 %shard_map.459 = (bf16[288,512]{1,0:T(8,128)(2,1)}, f32[288,512]{1,0:T(8,128)}, f32[288,512]{1,0:T(8,128)}, f32[32,512]{1,0:T(8,128)}, f32[32,512]{1,0:T(8,128)}...) custom-call(bf16[288,512]{1,0:T(8,128)(2,1)} %bitcast.41, f32[24,512]{1,0:T(8,128)} %shard_map.458.params_ref, ...), custom_call_target="tpu_custom_call" | custom-call | bytes 90000000 | tf_op jit(solution)/shard_map/pallas_call | solution.py:567
  38.7 7.3 %all-to-all-start = ((bf16[32,16,512]{2,1,0:T(8,128)(2,1)}), bf16[32,16,512]{2,1,0:T(8,128)(2,1)S(1)}, u32[]{:S(2)}, u32[]{:S(2)}) async-start(bf16[32,16,512]{2,1,0:T(8,128)(2,1)} %bitcast.44), calls=%async_computation | async-start | bytes 1048576 | tf_op jit(solution)/shard_map/all_to_all | solution.py:930
  46.1 27.9 %shard_map.461 = (bf16[288,512]{1,0:T(8,128)(2,1)}, f32[288,512]{1,0:T(8,128)}, f32[288,512]{1,0:T(8,128)}, f32[32,512]{1,0:T(8,128)}, f32[32,512]{1,0:T(8,128)}...) custom-call(bf16[288,512]{1,0:T(8,128)(2,1)} %bitcast.42, f32[24,512]{1,0:T(8,128)} %shard_map.458.params_ref, ...), custom_call_target="tpu_custom_call" | custom-call | bytes 90000000 | tf_op jit(solution)/shard_map/pallas_call | solution.py:567
  74.0 5.8 %all-to-all-start.1 = ((bf16[32,16,640]{2,1,0:T(8,128)(2,1)}), bf16[32,16,640]{2,1,0:T(8,128)(2,1)S(1)}, u32[]{:S(2)}, u32[]{:S(2)}) async-start(bf16[32,16,640]{2,1,0:T(8,128)(2,1)} %bitcast.43), calls=%async_computation.1 | async-start | bytes 1310720 | tf_op jit(solution)/shard_map/all_to_all | solution.py:930
  80.7 1.9 reshape.147.merge_ref
  82.7 0.7 fusion.3.mask_ref
  83.4 22.5 %shard_map.462 = (f32[288,512]{1,0:T(8,128)}, f32[288,1024]{1,0:T(8,128)}, bf16[5120,512]{1,0:T(8,128)(2,1)}, f32[10,512]{1,0:T(8,128)}) custom-call(bf16[288,512]{1,0:T(8,128)(2,1)} %shard_map.460.fine_ref, bf16[288,512]{1,0:T(8,128)(2,1)} %get-tuple-element.63.coarse_ref, bf16[1024,512]{1,0:T(8,128)(2,1)} %reshape.147.merge_ref, ...), custom_call_target="tpu_custom_call" | custom-call | bytes 70000000 | tf_op jit(solution)/shard_map/pallas_call | solution.py:859
  105.9 0.9 copy-done.1
  106.7 9.3 %shard_map.464 = (bf16[2048,512]{1,0:T(8,128)(2,1)}, bf16[512,512]{1,0:T(8,128)(2,1)}, bf16[512,512]{1,0:T(8,128)(2,1)}, f32[288,512]{1,0:T(8,128)}, f32[288,512]{1,0:T(8,128)}) custom-call(f32[288,1024]{1,0:T(8,128)} %shard_map.463.grad_ref, f32[288,512]{1,0:T(8,128)} %get-tuple-element.67.up_fine_ref, f32[288,512]{1,0:T(8,128)} %get-tuple-element.68.season_fine_ref, ...), custom_call_target="tpu_custom_call" | custom-call | bytes 100000 | tf_op jit(solution)/shard_map/pallas_call | solution.py:603
  116.0 5.8 %all-to-all-start.2 = ((bf16[32,64,512]{2,1,0:T(8,128)(2,1)}), bf16[32,64,512]{2,1,0:T(8,128)(2,1)S(1)}, u32[]{:S(2)}, u32[]{:S(2)}) async-start(bf16[32,64,512]{2,1,0:T(8,128)(2,1)} %bitcast.38), calls=%async_computation.2 | async-start | bytes 4194304 | tf_op jit(solution)/shard_map/all_to_all | solution.py:930
  122.1 21.3 %shard_map.466 = (bf16[48,512]{1,0:T(8,128)(2,1)}, bf16[32,512]{1,0:T(8,128)(2,1)}) custom-call(bf16[512,512]{1,0:T(8,128)(2,1)} %get-tuple-element.78.right_in_ref, f32[32,512]{1,0:T(8,128)} %get-tuple-element.79.down_out_ref, f32[32,512]{1,0:T(8,128)} %get-tuple-element.80.iso_out_ref, f32[24,512]{1,0:T(8,128)} %shard_map.458.params_ref, ...), custom_call_target="tpu_custom_call" | custom-call | bytes 80000000 | tf_op jit(solution)/shard_map/pallas_call | solution.py:632
  143.5 25.6 %shard_map.465 = (bf16[56,512]{1,0:T(8,128)(2,1)}, bf16[32,512]{1,0:T(8,128)(2,1)}) custom-call(bf16[512,512]{1,0:T(8,128)(2,1)} %get-tuple-element.74.right_in_ref, f32[32,512]{1,0:T(8,128)} %get-tuple-element.75.down_out_ref, f32[32,512]{1,0:T(8,128)} %get-tuple-element.76.iso_out_ref, f32[24,512]{1,0:T(8,128)} %shard_map.458.params_ref, ...), custom_call_target="tpu_custom_call" | custom-call | bytes 80000000 | tf_op jit(solution)/shard_map/pallas_call | solution.py:632
  169.1 1.5 pad_maximum_fusion.1.refs_0_
  170.7 1.4 copy-done
  172.1 1.1 convert_reduce_fusion.1
  173.2 2.3 fusion
  175.5 1.0 pad_maximum_fusion
  176.5 5.7 %all-to-all-start.3 = ((bf16[32,18,512]{2,1,0:T(8,128)(2,1)}), bf16[32,18,512]{2,1,0:T(8,128)(2,1)S(1)}, u32[]{:S(2)}, u32[]{:S(2)}) async-start(bf16[32,18,512]{2,1,0:T(8,128)(2,1)} %pad_maximum_fusion), calls=%async_computation.3 | async-start | bytes 1572864 | tf_op jit(solution)/shard_map/all_to_all | solution.py:930
  182.2 21.6 %shard_map.469.refs_1_ = f32[288,512]{1,0:T(8,128)} custom-call(bf16[32,512]{1,0:T(8,128)(2,1)} %get-tuple-element.77.grad_fine_ref, bf16[32,512]{1,0:T(8,128)(2,1)} %shard_map.468.grad_coarse_ref, f32[288,512]{1,0:T(8,128)} %get-tuple-element.85.outer_fine_ref, f32[288,512]{1,0:T(8,128)} %get-tuple-element.86.outer_coarse_ref, bf16[12,262144]{1,0:T(8,128)(2,1)} %fine_ref.1, ...), custom_call_target="tpu_custom_call" | custom-call | bytes 80000000 | tf_op jit(solution)/shard_map/pallas_call | solution.py:663
  203.8 1.1 all-to-all-done.3.refs_0_
  205.0 3.8 %all-to-all-start.4 = ((bf16[4,160,512]{2,1,0:T(8,128)(2,1)}), bf16[4,160,512]{2,1,0:T(8,128)(2,1)S(1)}, u32[]{:S(2)}, u32[]{:S(2)}) async-start(bf16[4,160,512]{2,1,0:T(8,128)(2,1)} %bitcast.39), calls=%async_computation.5 | async-start | bytes 1310720 | tf_op jit(solution)/shard_map/all_to_all | solution.py:900
  209.5 24.2 %all-to-all-done.4 = bf16[4,160,512]{2,1,0:T(8,128)(2,1)S(1)} async-done(((bf16[4,160,512]{2,1,0:T(8,128)(2,1)}), bf16[4,160,512]{2,1,0:T(8,128)(2,1)S(1)}, u32[]{:S(2)}, u32[]{:S(2)}) %all-to-all-start.4) | async-done | bytes 655392 | tf_op jit(solution)/shard_map/all_to_all | solution.py:900
  233.8 0.7 reshape.156
  234.4 0.7 fusion.5
  235.2 3.7 %all-gather.3.cloned.1.call-done = bf16[3328,512]{1,0:T(8,128)(2,1)} async-done(((bf16[104,512]{1,0:T(8,128)(2,1)}), bf16[3328,512]{1,0:T(8,128)(2,1)}) %all-gather.3.cloned.1.call-update) | async-done | bytes 3407888 | tf_op jit(solution)/shard_map/all_gather | solution.py:1143
  238.9 1.3 add_reduce_fusion
  240.2 0.6 fusion.6
  240.9 5.5 %shard_map.471 = (f32[16,8192]{1,0:T(8,128)}, f32[19,8192]{1,0:T(8,128)}, f32[2,512]{1,0:T(2,128)}, f32[12,8192]{1,0:T(8,128)}, f32[16,8192]{1,0:T(8,128)}) custom-call(bf16[32,16,640]{2,1,0:T(8,128)(2,1)} %copy-done.1, bf16[32,104,512]{2,1,0:T(8,128)(2,1)} %bitcast.36, bf16[32,18,512]{2,1,0:T(8,128)(2,1)} %copy-done.3), custom_call_target="tpu_custom_call" | custom-call | bytes 17000000 | tf_op jit(solution)/shard_map/pallas_call | solution.py:1029
  246.4 1.3 fusion.7
  247.8 4.8 %shard_map.470 = (f32[12,8192]{1,0:T(8,128)}, f32[25,8192]{1,0:T(8,128)}, f32[2,512]{1,0:T(2,128)}) custom-call(bf16[32,16,512]{2,1,0:T(8,128)(2,1)} %copy-done.2, bf16[32,104,512]{2,1,0:T(8,128)(2,1)} %bitcast.37), custom_call_target="tpu_custom_call" | custom-call | bytes 17000000 | tf_op jit(solution)/shard_map/pallas_call | solution.py:1029
  252.6 1.3 fusion.8
  (34 shorter events, 1.6 us)
Async XLA Ops:
  38.7 35.3 %all-to-all-start = ((bf16[32,16,512]{2,1,0:T(8,128)(2,1)}), bf16[32,16,512]{2,1,0:T(8,128)(2,1)S(1)}, u32[]{:S(2)}, u32[]{:S(2)}) async-start(bf16[32,16,512]{2,1,0:T(8,128)(2,1)} %bitcast.44), calls=%async_computation | async-start | bytes 1048576 | tf_op jit(solution)/shard_map/all_to_all | solution.py:930
  46.0 34.7 %copy-start.4 = (bf16[2,262144]{1,0:T(2,128)(2,1)S(1)}, bf16[2,262144]{1,0:T(2,128)(2,1)}, u32[]{:S(2)}) copy-start(bf16[2,262144]{1,0:T(2,128)(2,1)} %param.44) | copy-start | bytes 3145732
  74.0 9.4 %copy-start.2 = (bf16[32,16,512]{2,1,0:T(8,128)(2,1)}, bf16[32,16,512]{2,1,0:T(8,128)(2,1)S(1)}, u32[]{:S(2)}) copy-start(bf16[32,16,512]{2,1,0:T(8,128)(2,1)S(1)} %all-to-all-done.refs_1_.columns_ref) | copy-start | bytes 1572868
  74.0 31.9 %all-to-all-start.1 = ((bf16[32,16,640]{2,1,0:T(8,128)(2,1)}), bf16[32,16,640]{2,1,0:T(8,128)(2,1)S(1)}, u32[]{:S(2)}, u32[]{:S(2)}) async-start(bf16[32,16,640]{2,1,0:T(8,128)(2,1)} %bitcast.43), calls=%async_computation.1 | async-start | bytes 1310720 | tf_op jit(solution)/shard_map/all_to_all | solution.py:930
  79.8 124.0 %reduce-scatter.2.cloned.1.call-start = ((), (), s32[]{:S(2)}) async-start(), calls=%async_computation.6 | async-start | bytes 5898240 | tf_op jit(solution)/shard_map/reduce_scatter | solution.py:892
  105.8 0.9 copy-start.1
  116.0 54.7 %all-to-all-start.2 = ((bf16[32,64,512]{2,1,0:T(8,128)(2,1)}), bf16[32,64,512]{2,1,0:T(8,128)(2,1)S(1)}, u32[]{:S(2)}, u32[]{:S(2)}) async-start(bf16[32,64,512]{2,1,0:T(8,128)(2,1)} %bitcast.38), calls=%async_computation.2 | async-start | bytes 4194304 | tf_op jit(solution)/shard_map/all_to_all | solution.py:930
  121.9 117.0 %all-gather.3.cloned.1.call-start = ((), (), s32[]{:S(2)}) async-start(), calls=%async_computation.7 | async-start | bytes 3514368 | tf_op jit(solution)/shard_map/all_gather | solution.py:1143
  143.5 25.6 %copy-start.5 = (bf16[48,512]{1,0:T(8,128)(2,1)S(1)}, bf16[48,512]{1,0:T(8,128)(2,1)}, u32[]{:S(2)}) copy-start(bf16[48,512]{1,0:T(8,128)(2,1)} %get-tuple-element.83) | copy-start | bytes 147460
  170.7 1.4 copy-start
  176.5 28.4 %all-to-all-start.3 = ((bf16[32,18,512]{2,1,0:T(8,128)(2,1)}), bf16[32,18,512]{2,1,0:T(8,128)(2,1)S(1)}, u32[]{:S(2)}, u32[]{:S(2)}) async-start(bf16[32,18,512]{2,1,0:T(8,128)(2,1)} %pad_maximum_fusion), calls=%async_computation.3 | async-start | bytes 1572864 | tf_op jit(solution)/shard_map/all_to_all | solution.py:930
  205.0 35.9 %copy-start.3 = (bf16[32,18,512]{2,1,0:T(8,128)(2,1)}, bf16[32,18,512]{2,1,0:T(8,128)(2,1)S(1)}, u32[]{:S(2)}) copy-start(bf16[32,18,512]{2,1,0:T(8,128)(2,1)S(1)} %all-to-all-done.3.refs_0_) | copy-start | bytes 1769476
  205.0 28.7 %all-to-all-start.4 = ((bf16[4,160,512]{2,1,0:T(8,128)(2,1)}), bf16[4,160,512]{2,1,0:T(8,128)(2,1)S(1)}, u32[]{:S(2)}, u32[]{:S(2)}) async-start(bf16[4,160,512]{2,1,0:T(8,128)(2,1)} %bitcast.39), calls=%async_computation.5 | async-start | bytes 1310720 | tf_op jit(solution)/shard_map/all_to_all | solution.py:900
Sparse Core Ops, SparseCore 0:
  116.1 65.6 reduce-scatter.1
Sparse Core Ops, SparseCore 1:
  172.2 66.6 all-gather.2

commit v2 on v1

--- a/solution.py
+++ b/solution.py
@@ -43,8 +43,8 @@
     rows = min(8, taps - 8 * slab)
 
     def step(number, carry):
-        for inner in range(4):
-            pair = number * 4 + inner
+        for inner in range(8):
+            pair = number * 8 + inner
             start = pl.multiple_of(pair * 1024, 1024)
             values = weight_ref[8 * slab : 8 * slab + rows, pl.ds(start, 1024)].astype(FLOAT)
             if rows < 8:
@@ -54,7 +54,7 @@
             wide_ref[pl.ds(first, 16), :] = both.astype(BFLOAT)
         return carry
 
-    lax.fori_loop(0, 16, step, 0)
+    lax.fori_loop(0, 8, step, 0)
 
 
 def _statistics(values):

time: 263 us -> 259 us (0.985)
  Pallas kernels: 169 us -> 165 us
  transfers between devices with their start and end apart: 7 -> 7, of which waited for: 4 -> 4; matrix products, arithmetic and copies ran while one was open for 4% -> 4% of each run, Pallas kernels for 46% -> 45%
where the time goes in v2:
time: 259 us; the launch traced here: 258 us
  Pallas kernels  165 us (64%)
  waiting for transfers between devices  31.3 us (12%)
  starting transfers between devices  27.3 us (11%)
  between operations  16.3 us (6%)
  local copies, waits for them, and re-layouts  8.92 us (3%)
  other arithmetic  6.3 us (2%)
    pallas_call x2, Pallas kernels, forward_branch(): pl.pallas_call(partial(forward_kernel, kernel, steps, bias), grid=(12,),...  55.7 us
    pallas_call x2, Pallas kernels, inner_grads(): pl.pallas_call(partial(inner_kernel, steps, _pad8(kernel)), grid=(8,), in...  45 us
    all_to_all x1, waiting for transfers between devices, feed_sums(): lax.all_to_all(part.reshape(len(across[0]), -1, channels), 'dp', 0, 0, ax...  23.8 us
    all_to_all x4, starting transfers between devices, exchange(): return lax.all_to_all(values, 'dp', 0, 0, tiled=False)  23 us
    pallas_call x1, Pallas kernels, dense_block(): pl.pallas_call(partial(dense_kernel, devices), out_shape=shapes, scratch_...  22.5 us
    pallas_call x1, Pallas kernels, series_grads(): pl.pallas_call(partial(series_kernel, (K_A, K_B)), grid=(8,), in_specs=[_...  21 us
    pallas_call x2, Pallas kernels, weight_grads(): pl.pallas_call(partial(weight_kernel, kernel, steps, offset, first, len(t...  10.4 us
    pallas_call x1, Pallas kernels, outer_grads(): pl.pallas_call(partial(outer_kernel, devices, kernels), out_shape=shapes,...  9.29 us
  transfers between devices with their start and end apart: 7, of which 4 were waited for; matrix products, arithmetic and copies ran while one was open for 4% of the time, Pallas kernels for 45%

profile of v2, /device:TPU:0, one launch (start us, length us, event | category | flops | bytes accessed | tf_op | source)
XLA Modules:
  0.0 257.8 jit_solution(3179054395767606671)
XLA Ops:
  8.0 1.5 shard_map.458.params_ref
  9.5 28.5 %shard_map.459 = (bf16[288,512]{1,0:T(8,128)(2,1)}, f32[288,512]{1,0:T(8,128)}, f32[288,512]{1,0:T(8,128)}, f32[32,512]{1,0:T(8,128)}, f32[32,512]{1,0:T(8,128)}...) custom-call(bf16[288,512]{1,0:T(8,128)(2,1)} %bitcast.41, f32[24,512]{1,0:T(8,128)} %shard_map.458.params_ref, ...), custom_call_target="tpu_custom_call" | custom-call | bytes 90000000 | tf_op jit(solution)/shard_map/pallas_call | solution.py:567
  38.0 7.3 %all-to-all-start = ((bf16[32,16,512]{2,1,0:T(8,128)(2,1)}), bf16[32,16,512]{2,1,0:T(8,128)(2,1)S(1)}, u32[]{:S(2)}, u32[]{:S(2)}) async-start(bf16[32,16,512]{2,1,0:T(8,128)(2,1)} %bitcast.44), calls=%async_computation | async-start | bytes 1048576 | tf_op jit(solution)/shard_map/all_to_all | solution.py:930
  45.4 27.3 %shard_map.461 = (bf16[288,512]{1,0:T(8,128)(2,1)}, f32[288,512]{1,0:T(8,128)}, f32[288,512]{1,0:T(8,128)}, f32[32,512]{1,0:T(8,128)}, f32[32,512]{1,0:T(8,128)}...) custom-call(bf16[288,512]{1,0:T(8,128)(2,1)} %bitcast.42, f32[24,512]{1,0:T(8,128)} %shard_map.458.params_ref, ...), custom_call_target="tpu_custom_call" | custom-call | bytes 90000000 | tf_op jit(solution)/shard_map/pallas_call | solution.py:567
  72.6 5.8 %all-to-all-start.1 = ((bf16[32,16,640]{2,1,0:T(8,128)(2,1)}), bf16[32,16,640]{2,1,0:T(8,128)(2,1)S(1)}, u32[]{:S(2)}, u32[]{:S(2)}) async-start(bf16[32,16,640]{2,1,0:T(8,128)(2,1)} %bitcast.43), calls=%async_computation.1 | async-start | bytes 1310720 | tf_op jit(solution)/shard_map/all_to_all | solution.py:930
  79.4 1.9 reshape.147.merge_ref
  81.3 0.7 fusion.3.mask_ref
  82.0 22.5 %shard_map.462 = (f32[288,512]{1,0:T(8,128)}, f32[288,1024]{1,0:T(8,128)}, bf16[5120,512]{1,0:T(8,128)(2,1)}, f32[10,512]{1,0:T(8,128)}) custom-call(bf16[288,512]{1,0:T(8,128)(2,1)} %shard_map.460.fine_ref, bf16[288,512]{1,0:T(8,128)(2,1)} %get-tuple-element.63.coarse_ref, bf16[1024,512]{1,0:T(8,128)(2,1)} %reshape.147.merge_ref, ...), custom_call_target="tpu_custom_call" | custom-call | bytes 70000000 | tf_op jit(solution)/shard_map/pallas_call | solution.py:859
  104.5 0.9 copy-done.1
  105.3 9.3 %shard_map.464 = (bf16[2048,512]{1,0:T(8,128)(2,1)}, bf16[512,512]{1,0:T(8,128)(2,1)}, bf16[512,512]{1,0:T(8,128)(2,1)}, f32[288,512]{1,0:T(8,128)}, f32[288,512]{1,0:T(8,128)}) custom-call(f32[288,1024]{1,0:T(8,128)} %shard_map.463.grad_ref, f32[288,512]{1,0:T(8,128)} %get-tuple-element.67.up_fine_ref, f32[288,512]{1,0:T(8,128)} %get-tuple-element.68.season_fine_ref, ...), custom_call_target="tpu_custom_call" | custom-call | bytes 100000 | tf_op jit(solution)/shard_map/pallas_call | solution.py:603
  114.7 5.8 %all-to-all-start.2 = ((bf16[32,64,512]{2,1,0:T(8,128)(2,1)}), bf16[32,64,512]{2,1,0:T(8,128)(2,1)S(1)}, u32[]{:S(2)}, u32[]{:S(2)}) async-start(bf16[32,64,512]{2,1,0:T(8,128)(2,1)} %bitcast.38), calls=%async_computation.2 | async-start | bytes 4194304 | tf_op jit(solution)/shard_map/all_to_all | solution.py:930
  120.8 20.5 %shard_map.466 = (bf16[48,512]{1,0:T(8,128)(2,1)}, bf16[32,512]{1,0:T(8,128)(2,1)}) custom-call(bf16[512,512]{1,0:T(8,128)(2,1)} %get-tuple-element.78.right_in_ref, f32[32,512]{1,0:T(8,128)} %get-tuple-element.79.down_out_ref, f32[32,512]{1,0:T(8,128)} %get-tuple-element.80.iso_out_ref, f32[24,512]{1,0:T(8,128)} %shard_map.458.params_ref, ...), custom_call_target="tpu_custom_call" | custom-call | bytes 80000000 | tf_op jit(solution)/shard_map/pallas_call | solution.py:632
  141.3 24.5 %shard_map.465 = (bf16[56,512]{1,0:T(8,128)(2,1)}, bf16[32,512]{1,0:T(8,128)(2,1)}) custom-call(bf16[512,512]{1,0:T(8,128)(2,1)} %get-tuple-element.74.right_in_ref, f32[32,512]{1,0:T(8,128)} %get-tuple-element.75.down_out_ref, f32[32,512]{1,0:T(8,128)} %get-tuple-element.76.iso_out_ref, f32[24,512]{1,0:T(8,128)} %shard_map.458.params_ref, ...), custom_call_target="tpu_custom_call" | custom-call | bytes 80000000 | tf_op jit(solution)/shard_map/pallas_call | solution.py:632
  165.8 1.5 pad_maximum_fusion.1.refs_0_
  167.3 2.1 all-to-all-done.2.refs_1_
  169.4 1.4 copy-done
  170.8 1.1 convert_reduce_fusion.1
  171.9 2.3 fusion
  174.2 1.0 pad_maximum_fusion
  175.1 4.0 %all-to-all-start.3 = ((bf16[32,18,512]{2,1,0:T(8,128)(2,1)}), bf16[32,18,512]{2,1,0:T(8,128)(2,1)S(1)}, u32[]{:S(2)}, u32[]{:S(2)}) async-start(bf16[32,18,512]{2,1,0:T(8,128)(2,1)} %pad_maximum_fusion), calls=%async_computation.3 | async-start | bytes 1572864 | tf_op jit(solution)/shard_map/all_to_all | solution.py:930
  179.2 21.0 %shard_map.469.refs_1_ = f32[288,512]{1,0:T(8,128)} custom-call(bf16[32,512]{1,0:T(8,128)(2,1)} %get-tuple-element.77.grad_fine_ref, bf16[32,512]{1,0:T(8,128)(2,1)} %shard_map.468.grad_coarse_ref, f32[288,512]{1,0:T(8,128)} %get-tuple-element.85.outer_fine_ref, f32[288,512]{1,0:T(8,128)} %get-tuple-element.86.outer_coarse_ref, bf16[12,262144]{1,0:T(8,128)(2,1)} %fine_ref.1, ...), custom_call_target="tpu_custom_call" | custom-call | bytes 80000000 | tf_op jit(solution)/shard_map/pallas_call | solution.py:663
  200.2 1.8 all-to-all-done.3.refs_0_
  202.0 3.7 %all-to-all-start.4 = ((bf16[4,160,512]{2,1,0:T(8,128)(2,1)}), bf16[4,160,512]{2,1,0:T(8,128)(2,1)S(1)}, u32[]{:S(2)}, u32[]{:S(2)}) async-start(bf16[4,160,512]{2,1,0:T(8,128)(2,1)} %bitcast.39), calls=%async_computation.5 | async-start | bytes 1310720 | tf_op jit(solution)/shard_map/all_to_all | solution.py:900
  206.4 23.8 %all-to-all-done.4 = bf16[4,160,512]{2,1,0:T(8,128)(2,1)S(1)} async-done(((bf16[4,160,512]{2,1,0:T(8,128)(2,1)}), bf16[4,160,512]{2,1,0:T(8,128)(2,1)S(1)}, u32[]{:S(2)}, u32[]{:S(2)}) %all-to-all-start.4) | async-done | bytes 655392 | tf_op jit(solution)/shard_map/all_to_all | solution.py:900
  230.3 0.7 reshape.156
  231.0 0.7 fusion.5
  231.7 3.6 %all-gather.3.cloned.1.call-done = bf16[3328,512]{1,0:T(8,128)(2,1)} async-done(((bf16[104,512]{1,0:T(8,128)(2,1)}), bf16[3328,512]{1,0:T(8,128)(2,1)}) %all-gather.3.cloned.1.call-update) | async-done | bytes 3407888 | tf_op jit(solution)/shard_map/all_gather | solution.py:1143
  235.3 1.3 add_reduce_fusion
  237.3 5.5 %shard_map.471 = (f32[16,8192]{1,0:T(8,128)}, f32[19,8192]{1,0:T(8,128)}, f32[2,512]{1,0:T(2,128)}, f32[12,8192]{1,0:T(8,128)}, f32[16,8192]{1,0:T(8,128)}) custom-call(bf16[32,16,640]{2,1,0:T(8,128)(2,1)} %copy-done.1, bf16[32,104,512]{2,1,0:T(8,128)(2,1)} %bitcast.36, bf16[32,18,512]{2,1,0:T(8,128)(2,1)} %copy-done.3), custom_call_target="tpu_custom_call" | custom-call | bytes 17000000 | tf_op jit(solution)/shard_map/pallas_call | solution.py:1029
  242.8 1.3 fusion.7
  244.2 4.8 %shard_map.470 = (f32[12,8192]{1,0:T(8,128)}, f32[25,8192]{1,0:T(8,128)}, f32[2,512]{1,0:T(2,128)}) custom-call(bf16[32,16,512]{2,1,0:T(8,128)(2,1)} %copy-done.2, bf16[32,104,512]{2,1,0:T(8,128)(2,1)} %bitcast.37), custom_call_target="tpu_custom_call" | custom-call | bytes 17000000 | tf_op jit(solution)/shard_map/pallas_call | solution.py:1029
  249.0 1.3 fusion.8
  (34 shorter events, 2.0 us)
Async XLA Ops:
  38.0 34.6 %all-to-all-start = ((bf16[32,16,512]{2,1,0:T(8,128)(2,1)}), bf16[32,16,512]{2,1,0:T(8,128)(2,1)S(1)}, u32[]{:S(2)}, u32[]{:S(2)}) async-start(bf16[32,16,512]{2,1,0:T(8,128)(2,1)} %bitcast.44), calls=%async_computation | async-start | bytes 1048576 | tf_op jit(solution)/shard_map/all_to_all | solution.py:930
  45.4 34.0 %copy-start.4 = (bf16[2,262144]{1,0:T(2,128)(2,1)S(1)}, bf16[2,262144]{1,0:T(2,128)(2,1)}, u32[]{:S(2)}) copy-start(bf16[2,262144]{1,0:T(2,128)(2,1)} %param.44) | copy-start | bytes 3145732
  72.6 9.4 %copy-start.2 = (bf16[32,16,512]{2,1,0:T(8,128)(2,1)}, bf16[32,16,512]{2,1,0:T(8,128)(2,1)S(1)}, u32[]{:S(2)}) copy-start(bf16[32,16,512]{2,1,0:T(8,128)(2,1)S(1)} %all-to-all-done.refs_1_.columns_ref) | copy-start | bytes 1572868
  72.6 31.9 %all-to-all-start.1 = ((bf16[32,16,640]{2,1,0:T(8,128)(2,1)}), bf16[32,16,640]{2,1,0:T(8,128)(2,1)S(1)}, u32[]{:S(2)}, u32[]{:S(2)}) async-start(bf16[32,16,640]{2,1,0:T(8,128)(2,1)} %bitcast.43), calls=%async_computation.1 | async-start | bytes 1310720 | tf_op jit(solution)/shard_map/all_to_all | solution.py:930
  78.5 121.7 %reduce-scatter.2.cloned.1.call-start = ((), (), s32[]{:S(2)}) async-start(), calls=%async_computation.6 | async-start | bytes 5898240 | tf_op jit(solution)/shard_map/reduce_scatter | solution.py:892
  104.5 0.9 copy-start.1
  114.7 54.7 %all-to-all-start.2 = ((bf16[32,64,512]{2,1,0:T(8,128)(2,1)}), bf16[32,64,512]{2,1,0:T(8,128)(2,1)S(1)}, u32[]{:S(2)}, u32[]{:S(2)}) async-start(bf16[32,64,512]{2,1,0:T(8,128)(2,1)} %bitcast.38), calls=%async_computation.2 | async-start | bytes 4194304 | tf_op jit(solution)/shard_map/all_to_all | solution.py:930
  120.5 114.8 %all-gather.3.cloned.1.call-start = ((), (), s32[]{:S(2)}) async-start(), calls=%async_computation.7 | async-start | bytes 3514368 | tf_op jit(solution)/shard_map/all_gather | solution.py:1143
  141.3 24.5 %copy-start.5 = (bf16[48,512]{1,0:T(8,128)(2,1)S(1)}, bf16[48,512]{1,0:T(8,128)(2,1)}, u32[]{:S(2)}) copy-start(bf16[48,512]{1,0:T(8,128)(2,1)} %get-tuple-element.83) | copy-start | bytes 147460
  169.4 1.4 copy-start
  175.1 26.8 %all-to-all-start.3 = ((bf16[32,18,512]{2,1,0:T(8,128)(2,1)}), bf16[32,18,512]{2,1,0:T(8,128)(2,1)S(1)}, u32[]{:S(2)}, u32[]{:S(2)}) async-start(bf16[32,18,512]{2,1,0:T(8,128)(2,1)} %pad_maximum_fusion), calls=%async_computation.3 | async-start | bytes 1572864 | tf_op jit(solution)/shard_map/all_to_all | solution.py:930
  202.0 35.3 %copy-start.3 = (bf16[32,18,512]{2,1,0:T(8,128)(2,1)}, bf16[32,18,512]{2,1,0:T(8,128)(2,1)S(1)}, u32[]{:S(2)}) copy-start(bf16[32,18,512]{2,1,0:T(8,128)(2,1)S(1)} %all-to-all-done.3.refs_0_) | copy-start | bytes 1769476
  202.0 28.2 %all-to-all-start.4 = ((bf16[4,160,512]{2,1,0:T(8,128)(2,1)}), bf16[4,160,512]{2,1,0:T(8,128)(2,1)S(1)}, u32[]{:S(2)}, u32[]{:S(2)}) async-start(bf16[4,160,512]{2,1,0:T(8,128)(2,1)} %bitcast.39), calls=%async_computation.5 | async-start | bytes 1310720 | tf_op jit(solution)/shard_map/all_to_all | solution.py:900
Sparse Core Ops, SparseCore 0:
  114.8 65.6 reduce-scatter.1
Sparse Core Ops, SparseCore 1:
  170.9 64.4 all-gather.2
